TPU v7x, 32 devices: a whole 2x2x4 slice. The times are simulated.
32 devices in a mesh: dp: 16 (over z, y, x), mp: 2 (over core).
Axes of the slice: x: 2, y: 2, z: 4, core: 2. Of those that a mesh axis runs over, the one named last changes fastest.
Arguments:
- query: bfloat16 [1024, 4096], P('dp', 'mp'), may hold values from -144 to 144
- new_key: bfloat16 [1024, 4096], P('dp', 'mp'), may hold values from -6 to 6
- new_value: bfloat16 [1024, 4096], P('dp', 'mp'), may hold values from -6 to 6
- cache_key: bfloat16 [1024, 32, 16, 128], P('dp', 'mp'), may hold values from -6 to 6
- cache_value: bfloat16 [1024, 32, 16, 128], P('dp', 'mp'), may hold values from -6 to 6
- cache_len: int32 [1024], P('dp'), may hold values from 2 to 16
- residual: bfloat16 [1024, 8192], P('dp'), may hold values from -6 to 6
- out_weight: bfloat16 [4096, 8192], P('mp'), may hold values from -0.1875 to 0.1875
- norm_gain: bfloat16 [8192], P('mp'), may hold values from 0.25 to 1.75
- codec_weight: bfloat16 [8192, 1024], P('mp'), may hold values from -0.125 to 0.125
- finished: int32 [1024], P('dp'), may hold values from 0 to 1
- owner: int32 [1024], P('dp'), may hold values from 0 to 15, as said below
- frames: bfloat16 [16384, 1024], P('dp', 'mp'), may hold values from -6 to 6
- snake_alpha: float32 [1024], P('mp'), may hold values from 0.5 to 2
- filter_weight: bfloat16 [7, 1024, 1024], P(None, None, 'mp'), may hold values from -0.125 to 0.125
- conv_bias: float32 [1024], P('mp'), may hold values from -4 to 4
Outputs:
- hidden: bfloat16 [1024, 8192], P('dp', 'mp')
- audio: bfloat16 [16384, 1024], P('dp', 'mp')
Inputs may be any that keep to these rules, and one draw needn't show every extreme that they name: Within each aligned block of 64 rows, at most 4 finished rows name the same owner, and some owner is named by exactly 4 finished rows of the block.
All inputs are finite; a program needn't handle non-finite values.
Results may differ from a plain program's by a relative error of at most 0.0056.
Values may be sent and summed in bfloat16 or wider, within the bound.
A program may use at most 128 MiB of HBM per device.

v0:
```python
import jax
import jax.numpy as jnp
from jax import lax
from jax.sharding import PartitionSpec as P

KERNEL_TAPS = 7
DILATION_STEP = 3
CAP = 4


def padded(cells, sides, width):
    for axis, dim in sides:
        count = lax.axis_size(axis)
        ends = count - 1
        head = lax.slice_in_dim(cells, 0, width, axis=dim)
        tail = lax.slice_in_dim(cells, cells.shape[dim] - width, cells.shape[dim], axis=dim)
        cells = jnp.concatenate(
            [
                lax.ppermute(tail, axis, [(i, (i + 1) % count) for i in range(ends)]),
                cells,
                lax.ppermute(head, axis, [((i + 1) % count, i) for i in range(ends)]),
            ],
            axis=dim,
        )
    return cells


def attend(query, new_key, new_value, cache_key, cache_value, cache_len):
    count, heads, positions, depth = cache_key.shape
    scale = 1.0 / jnp.sqrt(jnp.float32(depth))
    queries = query.reshape(count, heads, depth)
    fresh_key = new_key.reshape(count, heads, depth)
    fresh_value = new_value.reshape(count, heads, depth)
    scores = (
        jnp.einsum("rhd,rhld->rhl", queries, cache_key, preferred_element_type=jnp.float32) * scale
    )
    own_score = (
        jnp.einsum("rhd,rhd->rh", queries, fresh_key, preferred_element_type=jnp.float32) * scale
    )
    valid = jnp.arange(positions, dtype=jnp.int32)[None, :] < cache_len[:, None]
    scores = jnp.where(valid[:, None, :], scores, -1e30)
    top = jnp.maximum(jnp.max(scores, axis=-1), own_score)
    expo = jnp.where(valid[:, None, :], jnp.exp(scores - top[..., None]), 0.0)
    own_expo = jnp.exp(own_score - top)
    total = jnp.sum(expo, axis=-1) + own_expo
    weights = (expo / total[..., None]).astype(jnp.bfloat16)
    own_weight = (own_expo / total).astype(jnp.bfloat16)
    mixed = jnp.einsum("rhl,rhld->rhd", weights, cache_value, preferred_element_type=jnp.float32)
    mixed = mixed + own_weight.astype(jnp.float32)[..., None] * fresh_value.astype(jnp.float32)
    return mixed.astype(jnp.bfloat16).reshape(count, heads * depth)


def body(
    query,
    new_key,
    new_value,
    cache_key,
    cache_value,
    cache_len,
    residual,
    out_weight,
    norm_gain,
    codec_weight,
    finished,
    owner,
    frames,
    snake_alpha,
    filter_weight,
    conv_bias,
):
    attended = attend(query, new_key, new_value, cache_key, cache_value, cache_len)
    count = attended.shape[0]
    width = out_weight.shape[1]
    local_width = norm_gain.shape[0]
    term = jnp.dot(attended, out_weight, preferred_element_type=jnp.float32)
    projected = lax.psum_scatter(term, "mp", scatter_dimension=1, tiled=True)
    residual_part = lax.dynamic_slice_in_dim(
        residual, lax.axis_index("mp") * local_width, local_width, 1
    )
    hidden = (residual_part.astype(jnp.float32) + projected).astype(jnp.bfloat16)
    wide = hidden.astype(jnp.float32)
    squares = lax.psum(jnp.sum(wide * wide, axis=-1), "mp")
    meansq = squares / width
    normed = (wide * norm_gain.astype(jnp.float32)).astype(jnp.bfloat16)
    partial_value = jnp.dot(normed, codec_weight, preferred_element_type=jnp.float32)
    latent = lax.psum_scatter(partial_value, "mp", scatter_dimension=1, tiled=True)
    latent = (latent * lax.rsqrt(meansq + 1e-05)[:, None]).astype(jnp.bfloat16)
    owners = lax.axis_size("dp")
    index = jnp.arange(count, dtype=jnp.int32)
    earlier = (
        (owner[:, None] == owner[None, :])
        & (finished[None, :] == 1)
        & (index[None, :] < index[:, None])
    )
    slot = jnp.sum(earlier.astype(jnp.int32), axis=1)
    target = owner * CAP + slot
    places = jnp.arange(owners * CAP, dtype=jnp.int32)
    onehot = ((places[:, None] == target[None, :]) & (finished[None, :] == 1)).astype(jnp.bfloat16)
    outgoing = jnp.dot(onehot, latent, preferred_element_type=jnp.float32).astype(jnp.bfloat16)
    outgoing = outgoing.reshape(owners, CAP, latent.shape[1])
    incoming = lax.all_to_all(outgoing, "dp", split_axis=0, concat_axis=0, tiled=True)
    incoming = incoming.reshape(owners * CAP, latent.shape[1]).astype(jnp.float32)
    frame_tally = frames.shape[0]
    incoming = jnp.pad(incoming, ((0, frame_tally - owners * CAP), (0, 0)))
    mix = frames.astype(jnp.float32) + incoming
    act = (mix + jnp.sin(snake_alpha * mix) ** 2 / snake_alpha).astype(jnp.bfloat16)
    filter_span = KERNEL_TAPS // 2 * DILATION_STEP
    channels = lax.all_gather(act, "mp", axis=1, tiled=True)
    padded_frames = padded(channels, (("dp", 0),), filter_span)
    dilated_filter = jnp.zeros(mix.shape, jnp.float32)
    for tap_index in range(KERNEL_TAPS):
        dilated_filter = dilated_filter + jnp.dot(
            padded_frames[tap_index * DILATION_STEP : tap_index * DILATION_STEP + frame_tally],
            filter_weight[tap_index],
            preferred_element_type=jnp.float32,
        )
    audio = (mix + conv_bias + dilated_filter).astype(jnp.bfloat16)
    return (hidden, audio)


def solution(mesh):
    placed = (
        P("dp", "mp"),
        P("dp", "mp"),
        P("dp", "mp"),
        P("dp", "mp", None, None),
        P("dp", "mp", None, None),
        P("dp"),
        P("dp", None),
        P("mp", None),
        P("mp"),
        P("mp", None),
        P("dp"),
        P("dp"),
        P("dp", "mp"),
        P("mp"),
        P(None, None, "mp"),
        P("mp"),
    )
    return jax.shard_map(
        body, mesh=mesh, in_specs=placed, out_specs=(P("dp", "mp"), P("dp", "mp")), check_vma=False
    )
```

profile of v0, /device:TPU:0, one launch (start us, length us, event | category | flops | bytes accessed | tf_op | source)
XLA Modules:
  0.0 123.1 jit_solution(5842894470540036404)
XLA Ops:
  7.2 0.7 iota_compare_fusion.2
  7.9 1.0 copy.29
  8.9 1.3 %reshape.63 = bf16[64,16,128,1]{2,3,1,0:T(2,128)(2,1)S(1)} reshape(bf16[64,2048]{1,0:T(8,128)(2,1)} %param.16) | data formatting | bytes 524288 | tf_op jit(solution)/shard_map/reshape | solution.py:31
  10.3 1.0 copy.28
  11.3 0.2 fusion.43
  11.7 4.4 %fusion.64 = f32[64,16,1,16]{3,2,1,0:T(1,128)S(1)} fusion(bf16[64,16,128,1]{2,3,1,0:T(2,128)(2,1)S(1)} %reshape.63, bf16[64,16,16,128]{3,2,1,0:T(8,128)(2,1)} %param.19), kind=kOutput, calls=%fused_computation.85 | convolution fusion | flops 4194304 | bytes 4521984 | tf_op jit(solution)/shard_map/rhd,rhld->rhl/dot_general | solution.py:35
  16.1 0.3 copy.20
  16.7 0.5 copy.25
  17.2 3.4 %fusion.65 = f32[64,16,1,128]{3,2,1,0:T(1,128)S(1)} fusion(bf16[64,16,16,1]{2,3,1,0:T(2,128)(2,1)S(1)} %copy.25, bf16[64,16,16,128]{3,2,1,0:T(8,128)(2,1)} %param.20), kind=kOutput, calls=%fused_computation.86 | convolution fusion | flops 4194304 | bytes 4751360 | tf_op jit(solution)/shard_map/rhl,rhld->rhd/dot_general | solution.py:48
  20.7 0.2 fusion.42
  20.9 14.9 %fusion.45 = f32[64,8192]{1,0:T(8,128)} fusion(bf16[2048,8192]{1,0:T(8,128)(2,1)} %param.23, bf16[8,8,16,128]{3,2,1,0:T(8,128)(2,1)S(1)} %bitcast.64), kind=kOutput, calls=%fused_computation.51 | convolution fusion | flops 2147483648 | bytes 35913728 | tf_op jit(solution)/shard_map/dot_general | solution.py:75
  35.9 0.6 copy-done.5
  36.5 12.0 %reduce-scatter.3.cloned.1.call-done = f32[64,4096]{1,0:T(8,128)} async-done(((f32[64,8192]{1,0:T(8,128)}), f32[64,4096]{1,0:T(8,128)}) %reduce-scatter.3.cloned.1.call-update) | async-done | bytes 1048592 | tf_op jit(solution)/shard_map/reduce_scatter | solution.py:76
  48.5 1.5 %fusion.19 = (f32[64]{0:T(128)S(1)}, bf16[64,4096]{1,0:T(8,128)(2,1)S(1)}) fusion(f32[64,4096]{1,0:T(8,128)} %reduce-scatter.3.cloned.1.call-done, bf16[64,8192]{1,0:T(8,128)(2,1)S(1)} %copy-done.4, s32[]{:T(128)S(6)} %select_n.10), kind=kLoop, calls=%fused_computation.26 | loop fusion | flops 1572800 | bytes 2097412 | tf_op jit(solution)/shard_map/reduce_sum | solution.py:82
  50.0 5.9 %fusion.39 = f32[64,1024]{1,0:T(8,128)} fusion(bf16[4096,1024]{1,0:T(8,128)(2,1)} %param.25, bf16[64,4096]{1,0:T(8,128)(2,1)S(1)} %get-tuple-element.3, f32[4096]{0:T(1024)S(1)} %convert_element_type.69), kind=kOutput, calls=%fused_computation.43 | convolution fusion | flops 537657344 | bytes 9191424 | tf_op jit(solution)/shard_map/dot_general | solution.py:85
  56.1 2.5 %psum.7 = f32[64]{0:T(128)S(1)} all-reduce(f32[64]{0:T(128)S(1)} %get-tuple-element.2), channel_id=1, replica_groups=mesh['dp'=16,'mp'=2] {'mp'}, use_global_device_ids=true, to_apply=%region_6.7 | all-reduce | flops 64 | bytes 512 | tf_op jit(solution)/shard_map/psum | solution.py:82
  58.6 6.4 %reduce-scatter.5.cloned.1.call-done = f32[64,512]{1,0:T(8,128)} async-done(((f32[64,1024]{1,0:T(8,128)}), f32[64,512]{1,0:T(8,128)}) %reduce-scatter.5.cloned.1.call-update) | async-done | bytes 131088 | tf_op jit(solution)/shard_map/reduce_scatter | solution.py:86
  65.1 1.1 convolution_convert_fusion
  66.2 14.1 %all_to_all.5 = bf16[16,4,512]{2,1,0:T(4,128)(2,1)S(1)} all-to-all(bf16[16,4,512]{2,1,0:T(4,128)(2,1)S(1)} %reshape.54), channel_id=1, replica_groups=mesh['dp'=16,'mp'=2] {'dp'}, dimensions={0} | all-to-all | bytes 131072 | tf_op jit(solution)/shard_map/all_to_all | solution.py:101
  80.3 7.9 %add_convert_fusion.1 = bf16[1024,512]{1,0:T(8,128)(2,1)} fusion(bf16[1024,512]{1,0:T(8,128)(2,1)S(1)} %copy-done.1, bf16[64,512]{1,0:T(8,128)(2,1)S(1)} %convert_element_type.73, f32[512]{0:T(512)S(1)} %copy-done.6), kind=kLoop, calls=%fused_computation.18 | loop fusion | flops 4194304 | bytes 2164736 | tf_op jit(solution)/shard_map/convert_element_type | solution.py:106
  88.2 7.5 %all-gather.2.cloned.1.call-done = bf16[1024,1024]{1,0:T(8,128)(2,1)} async-done(((bf16[1024,512]{1,0:T(8,128)(2,1)}), bf16[1024,1024]{1,0:T(8,128)(2,1)}) %all-gather.2.cloned.1.call-update) | async-done | bytes 2097168 | tf_op jit(solution)/shard_map/all_gather | solution.py:108
  95.7 0.8 fusion.63
  96.5 3.6 %collective-permute-start = (bf16[9,1024]{1,0:T(8,128)(2,1)S(1)}, bf16[9,1024]{1,0:T(8,128)(2,1)S(1)}, u32[]{:S(2)}, u32[]{:S(2)}) collective-permute-start(bf16[9,1024]{1,0:T(8,128)(2,1)S(1)} %get-tuple-element.4), channel_id=1, source_target_pairs={{0,2},{2,4},{4,6},{6,8},{8,10},{10,12},{12,14},{14,16},{16,18},{18... | collective-permute-start | bytes 55304 | tf_op jit(solution)/shard_map/ppermute | solution.py:19
  100.1 1.6 %collective-permute-start.1 = (bf16[9,1024]{1,0:T(8,128)(2,1)S(1)}, bf16[9,1024]{1,0:T(8,128)(2,1)S(1)}, u32[]{:S(2)}, u32[]{:S(2)}) collective-permute-start(bf16[9,1024]{1,0:T(8,128)(2,1)S(1)} %get-tuple-element.5), channel_id=1, source_target_pairs={{2,0},{4,2},{6,4},{8,6},{10,8},{12,10},{14,12},{16,14},{18,16},{20... | collective-permute-start | bytes 55304 | tf_op jit(solution)/shard_map/ppermute | solution.py:21
  101.8 3.1 %fusion.23 = f32[1024,512]{1,0:T(8,128)S(1)} fusion(bf16[1024,1024]{1,0:T(8,128)(2,1)} %all-gather.2.cloned.1.call-done, bf16[7,1024,512]{2,1,0:T(8,128)(2,1)} %param.30), kind=kOutput, calls=%fused_computation.30 | convolution fusion | flops 1073741824 | bytes 5242880 | tf_op jit(solution)/shard_map/dot_general | solution.py:112
  105.1 1.0 collective-permute-done.1
  106.1 2.6 %fusion.8 = f32[1024,512]{1,0:T(8,128)S(1)} fusion(bf16[1033,1024]{1,0:T(8,128)(2,1)S(1)} %constant_dynamic-update-slice_fusion, bf16[7,1024,512]{2,1,0:T(8,128)(2,1)} %param.30), kind=kOutput, calls=%fused_computation.8 | convolution fusion | flops 1073741824 | bytes 5242880 | tf_op jit(solution)/shard_map/dot_general | solution.py:112
  108.7 1.2 %fusion.10 = f32[1024,512]{1,0:T(8,128)S(1)} fusion(bf16[1033,1024]{1,0:T(8,128)(2,1)S(1)} %constant_dynamic-update-slice_fusion, bf16[7,1024,512]{2,1,0:T(8,128)(2,1)S(1)} %bitcast.71), kind=kOutput, calls=%fused_computation.10 | convolution fusion | flops 1073741824 | bytes 5242880 | tf_op jit(solution)/shard_map/dot_general | solution.py:112
  110.0 1.2 %fusion.4 = f32[1024,512]{1,0:T(8,128)S(1)} fusion(bf16[9,1024]{1,0:T(8,128)(2,1)S(1)} %collective-permute-done, bf16[1024,1024]{1,0:T(8,128)(2,1)S(1)} %copy-done.2, bf16[7,1024,512]{2,1,0:T(8,128)(2,1)S(1)} %bitcast.71), kind=kOutput, calls=%fused_computation.5 | convolution fusion | flops 1077936128 | bytes 5275648 | tf_op jit(solution)/shard_map/dot_general | solution.py:112
  111.3 1.2 %fusion.12 = f32[1024,512]{1,0:T(8,128)S(1)} fusion(bf16[1024,1024]{1,0:T(8,128)(2,1)S(1)} %copy-done.2, bf16[9,1024]{1,0:T(8,128)(2,1)S(1)} %collective-permute-done, bf16[7,1024,512]{2,1,0:T(8,128)(2,1)S(1)} %bitcast.71), kind=kOutput, calls=%fused_computation.13 | convolution fusion | flops 1077936128 | bytes 5275648 | tf_op jit(solution)/shard_map/dot_general | solution.py:112
  112.5 1.2 %fusion.1 = f32[1024,512]{1,0:T(8,128)S(1)} fusion(bf16[9,1024]{1,0:T(8,128)(2,1)S(1)} %collective-permute-done, bf16[1024,1024]{1,0:T(8,128)(2,1)S(1)} %copy-done.2, bf16[7,1024,512]{2,1,0:T(8,128)(2,1)S(1)} %bitcast.71), kind=kOutput, calls=%fused_computation.3 | convolution fusion | flops 1077936128 | bytes 5275648 | tf_op jit(solution)/shard_map/dot_general | solution.py:112
  113.8 2.7 %add_convert_fusion = bf16[1024,512]{1,0:T(8,128)(2,1)} fusion(f32[1024,512]{1,0:T(8,128)S(1)} %fusion.8, f32[1024,512]{1,0:T(8,128)S(1)} %fusion.10, f32[1024,512]{1,0:T(8,128)S(1)} %fusion.23, f32[1024,512]{1,0:T(8,128)S(1)} %fusion.12, f32[1024,512]{1,0:T(8,128)S(1)} %fusion.4, f32[1024,512]{1,0:T(8,128)S(1)} %fusion.1, ...), kind=kOutput, calls=%fused_computation.17 | convolution fusion | flops 1080033280 | bytes 17893376 | tf_op jit(solution)/shard_map/dot_general | solution.py:112
  (49 shorter events, 1.1 us)
Async XLA Ops:
  7.2 4.4 %copy-start.3 = (bf16[64,2048]{1,0:T(8,128)(2,1)S(1)}, bf16[64,2048]{1,0:T(8,128)(2,1)}, u32[]{:S(2)}) copy-start(bf16[64,2048]{1,0:T(8,128)(2,1)} %param.18) | copy-start | bytes 786436
  7.2 41.3 %reduce-scatter.3.cloned.1.call-start = ((), (), s32[]{:S(2)}) async-start(), calls=%async_computation.3 | async-start | bytes 3145728 | tf_op jit(solution)/shard_map/reduce_scatter | solution.py:76
  35.8 0.7 copy-start.5
  35.8 0.7 copy-start.9
  35.8 12.7 %copy-start.4 = (bf16[64,8192]{1,0:T(8,128)(2,1)S(1)}, bf16[64,8192]{1,0:T(8,128)(2,1)}, u32[]{:S(2)}) copy-start(bf16[64,8192]{1,0:T(8,128)(2,1)} %param.22) | copy-start | bytes 3145732
  35.8 29.2 %reduce-scatter.5.cloned.1.call-start = ((), (), s32[]{:S(2)}) async-start(), calls=%async_computation.4 | async-start | bytes 393216 | tf_op jit(solution)/shard_map/reduce_scatter | solution.py:86
  50.0 5.9 %copy-start = (bf16[64,4096]{1,0:T(8,128)(2,1)}, bf16[64,4096]{1,0:T(8,128)(2,1)S(1)}, u32[]{:S(2)}) copy-start(bf16[64,4096]{1,0:T(8,128)(2,1)S(1)} %get-tuple-element.3) | copy-start | bytes 1572868
  50.0 6.0 %copy-start.8 = (s32[64]{0:T(128)S(1)}, s32[64]{0:T(128)}, u32[]{:S(2)}) copy-start(s32[64]{0:T(128)} %param.27) | copy-start | bytes 772
  50.0 30.3 %copy-start.1 = (bf16[1024,512]{1,0:T(8,128)(2,1)S(1)}, bf16[1024,512]{1,0:T(8,128)(2,1)}, u32[]{:S(2)}) copy-start(bf16[1024,512]{1,0:T(8,128)(2,1)} %param.28) | copy-start | bytes 3145732
  50.0 30.3 %copy-start.6 = (f32[512]{0:T(512)S(1)}, f32[512]{0:T(512)}, u32[]{:S(2)}) copy-start(f32[512]{0:T(512)} %param.29) | copy-start | bytes 6148
  55.9 39.8 %all-gather.2.cloned.1.call-start = ((), (), s32[]{:S(2)}) async-start(), calls=%async_computation.5 | async-start | bytes 3145728 | tf_op jit(solution)/shard_map/all_gather | solution.py:108
  96.5 13.5 %collective-permute-start = (bf16[9,1024]{1,0:T(8,128)(2,1)S(1)}, bf16[9,1024]{1,0:T(8,128)(2,1)S(1)}, u32[]{:S(2)}, u32[]{:S(2)}) collective-permute-start(bf16[9,1024]{1,0:T(8,128)(2,1)S(1)} %get-tuple-element.4), channel_id=1, source_target_pairs={{0,2},{2,4},{4,6},{6,8},{8,10},{10,12},{12,14},{14,16},{16,18},{18... | collective-permute-start | bytes 55304 | tf_op jit(solution)/shard_map/ppermute | solution.py:19
  100.1 4.7 %copy-start.2 = (bf16[1024,1024]{1,0:T(8,128)(2,1)S(1)}, bf16[1024,1024]{1,0:T(8,128)(2,1)}, u32[]{:S(2)}) copy-start(bf16[1024,1024]{1,0:T(8,128)(2,1)} %all-gather.2.cloned.1.call-done) | copy-start | bytes 6291460
  100.1 5.9 %collective-permute-start.1 = (bf16[9,1024]{1,0:T(8,128)(2,1)S(1)}, bf16[9,1024]{1,0:T(8,128)(2,1)S(1)}, u32[]{:S(2)}, u32[]{:S(2)}) collective-permute-start(bf16[9,1024]{1,0:T(8,128)(2,1)S(1)} %get-tuple-element.5), channel_id=1, source_target_pairs={{2,0},{4,2},{6,4},{8,6},{10,8},{12,10},{14,12},{16,14},{18,16},{20... | collective-permute-start | bytes 55304 | tf_op jit(solution)/shard_map/ppermute | solution.py:21
  104.9 3.8 %slice-start = ((s8[7340032]{0:T(1024)(128)(4,1)}), s8[4194304]{0:T(1024)(128)(4,1)S(1)}, s32[]{:S(2)}) async-start(s8[7340032]{0:T(1024)(128)(4,1)} %bitcast.70), calls=%async_computation.6 | async-start | bytes 8388608
  106.1 2.6 %slice-start.1 = ((s8[7340032]{0:T(1024)(128)(4,1)}), s8[3145728]{0:T(1024)(128)(4,1)S(1)}, s32[]{:S(2)}) async-start(s8[7340032]{0:T(1024)(128)(4,1)} %bitcast.70), calls=%async_computation.7 | async-start | bytes 6291456
  112.5 1.3 %copy-start.7 = (f32[512]{0:T(512)S(1)}, f32[512]{0:T(512)}, u32[]{:S(2)}) copy-start(f32[512]{0:T(512)} %param.31) | copy-start | bytes 6148
Sparse Core Ops, SparseCore 0:
  36.0 12.4 reduce-scatter.2
  56.0 8.9 reduce-scatter.4
  88.3 7.3 all-gather.1
where the time goes:
time: 125 us; the launch traced here: 123 us
  matrix products  43.2 us (35%)
  waiting for transfers between devices  26.9 us (22%)
  blocking collectives  16.5 us (13%)
  between operations  14.1 us (11%)
  other arithmetic  10.9 us (9%)
  local copies, waits for them, and re-layouts  6.04 us (5%)
  starting transfers between devices  5.37 us (4%)
    dot_general x1, matrix products, body(): term = jnp.dot(attended, out_weight, preferred_element_type=jnp.float32)  14.9 us
    all_to_all x1, blocking collectives, body(): lax.all_to_all(outgoing, 'dp', split_axis=0, concat_axis=0, tiled=True)  14.1 us
    dot_general x7, matrix products, body(): jnp.dot(padded_frames[tap_index * DILATION_STEP:tap_index * DILATION_STEP...  13.5 us
    reduce_scatter x1, waiting for transfers between devices, body(): projected = lax.psum_scatter(term, 'mp', scatter_dimension=1, tiled=True)  12 us
    convert_element_type x1, other arithmetic, body(): (mix + jnp.sin(snake_alpha * mix) ** 2 / snake_alpha).astype(jnp.bfloat16)  7.87 us
    all_gather x1, waiting for transfers between devices, body(): channels = lax.all_gather(act, 'mp', axis=1, tiled=True)  7.49 us
    reduce_scatter x1, waiting for transfers between devices, body(): lax.psum_scatter(partial_value, 'mp', scatter_dimension=1, tiled=True)  6.43 us
    dot_general x1, matrix products, body(): jnp.dot(normed, codec_weight, preferred_element_type=jnp.float32)  5.86 us
  transfers between devices with their start and end apart: 5, of which 4 were waited for; matrix products, arithmetic and copies ran while one was open for 6% of the time, Pallas kernels for 0%

commit v1 on v0

v1 whole, which is shorter than its diff:
```python
import functools
import jax
import jax.numpy as jnp
from jax import lax
from jax.experimental import pallas as pl
from jax.experimental.pallas import tpu as pltpu
from jax.sharding import PartitionSpec as P

KERNEL_TAPS = 7
DILATION_STEP = 3
CAP = 4
ROW_TILE = 16


def swap(x):
    return lax.ppermute(x, "mp", [(0, 1), (1, 0)])


def gather_mp(x, axis):
    if lax.axis_size("mp") != 2:
        return lax.all_gather(x, "mp", axis=axis, tiled=True)
    other = swap(x)
    first = lax.axis_index("mp") == 0
    return jnp.concatenate([jnp.where(first, x, other), jnp.where(first, other, x)], axis=axis)


def sin_squared(x):
    turns = jnp.round(x * 0.3183098861837907)
    r = (x - turns * 3.140625) - turns * 0.0009676535897932
    q = r * r
    p = -2.5052108e-08 + q * 1.6059044e-10
    p = 2.7557319e-06 + q * p
    p = -1.9841270e-04 + q * p
    p = 8.3333333e-03 + q * p
    p = -1.6666667e-01 + q * p
    sine = r + r * (q * p)
    return sine * sine


def snake(mix, alpha):
    return (mix + sin_squared(alpha * mix) / alpha).astype(jnp.bfloat16)


def columns_kernel(start_ref, x_ref, w_ref, o_ref):
    del start_ref
    o_ref[...] = jnp.dot(x_ref[...], w_ref[...], preferred_element_type=jnp.float32).astype(
        o_ref.dtype
    )


def columns_dot(x, w, start, width, tile, dtype):
    rows, depth = x.shape
    return pl.pallas_call(
        columns_kernel,
        out_shape=jax.ShapeDtypeStruct((rows, width), dtype),
        grid_spec=pltpu.PrefetchScalarGridSpec(
            num_scalar_prefetch=1,
            grid=(width // tile,),
            in_specs=[
                pl.BlockSpec((rows, depth), lambda j, s: (0, 0)),
                pl.BlockSpec((depth, tile), lambda j, s: (0, s[0] + j)),
            ],
            out_specs=pl.BlockSpec((rows, tile), lambda j, s: (0, j)),
        ),
        compiler_params=pltpu.CompilerParams(vmem_limit_bytes=28 * 1024 * 1024),
        cost_estimate=pl.CostEstimate(
            flops=2 * rows * depth * width, bytes_accessed=2 * depth * width, transcendentals=0
        ),
    )(jnp.full((1,), start, jnp.int32), x, w)


def handoff_kernel(
    n_dp, n_mp, near, out_ref, a_ref, b_ref, land_a, land_b, send_a, recv_a, send_b, recv_b
):
    dp = lax.axis_index("dp")
    mp = lax.axis_index("mp")
    count = n_dp * n_mp
    me = dp * n_mp + mp
    barrier = pltpu.get_barrier_semaphore()

    def place(step):
        peer = lax.rem(me + step, count)
        return peer, peer // n_mp, lax.rem(peer, n_mp)

    def greet(step, carry):
        _, pd, pm = place(step)
        pl.semaphore_signal(
            barrier, inc=1, device_id=(pd, pm), device_id_type=pl.DeviceIdType.MESH
        )
        return carry

    lax.fori_loop(1, count, greet, 0)
    pl.semaphore_wait(barrier, count - 1)

    def copy_a(pd, pm, send, recv):
        return pltpu.make_async_remote_copy(
            src_ref=out_ref.at[pd],
            dst_ref=land_a.at[me],
            send_sem=send_a.at[send],
            recv_sem=recv_a.at[recv],
            device_id=(pd, pm),
            device_id_type=pl.DeviceIdType.MESH,
        )

    def copy_b(slot, pd, pm, send, recv):
        return pltpu.make_async_remote_copy(
            src_ref=out_ref.at[pd + 1],
            dst_ref=land_b.at[slot],
            send_sem=send_b.at[send],
            recv_sem=recv_b.at[recv],
            device_id=(pd, pm),
            device_id_type=pl.DeviceIdType.MESH,
        )

    def send(step, carry):
        peer, pd, pm = place(step)
        copy_a(pd, pm, peer, me).start()
        return carry

    def send_near(step, carry):
        peer, pd, pm = place(step)
        copy_b(me, pd, pm, peer, me).start()
        return carry

    @pl.when(dp < near)
    def _():
        lax.fori_loop(1, count, send_near, 0)

    lax.fori_loop(1, count, send, 0)
    land_a[me] = out_ref[dp]

    @pl.when(dp < near)
    def _():
        land_b[me] = out_ref[dp + 1]

    def finish(step, carry):
        peer, pd, pm = place(step)
        copy = copy_a(pd, pm, peer, peer)
        copy.wait_recv()
        copy.wait_send()
        return carry

    def finish_near(step, carry):
        peer, pd, pm = place(step)
        copy_b(me, pd, pm, peer, me).wait_send()
        return carry

    def take_near(sender, carry):
        @pl.when(sender != me)
        def _():
            copy_b(sender, 0, 0, sender, sender).wait_recv()

        return carry

    lax.fori_loop(1, count, finish, 0)

    @pl.when(dp < near)
    def _():
        lax.fori_loop(1, count, finish_near, 0)

    lax.fori_loop(0, near * n_mp, take_near, 0)

    def total_of(land, first):
        total = land[first].astype(jnp.float32)
        for m in range(1, n_mp):
            total = total + land[first + m].astype(jnp.float32)
        return total

    def put(d, carry):
        a_ref[d] = total_of(land_a, d * n_mp)
        return carry

    lax.fori_loop(0, n_dp, put, 0)
    for d in range(near):
        b_ref[d] = total_of(land_b, d * n_mp)


def handoff(outgoing, near):
    n_dp, n_mp = lax.axis_size("dp"), lax.axis_size("mp")
    count = n_dp * n_mp
    _, cap, width = outgoing.shape
    vmem = pl.BlockSpec(memory_space=pltpu.VMEM)
    return pl.pallas_call(
        functools.partial(handoff_kernel, n_dp, n_mp, near),
        out_shape=(
            jax.ShapeDtypeStruct((n_dp, cap, width), jnp.float32),
            jax.ShapeDtypeStruct((near, cap, width), jnp.float32),
        ),
        in_specs=[vmem],
        out_specs=(vmem, vmem),
        scratch_shapes=[
            pltpu.VMEM((count, cap, width), jnp.bfloat16),
            pltpu.VMEM((near * n_mp, cap, width), jnp.bfloat16),
            pltpu.SemaphoreType.DMA((count,)),
            pltpu.SemaphoreType.DMA((count,)),
            pltpu.SemaphoreType.DMA((count,)),
            pltpu.SemaphoreType.DMA((near * n_mp,)),
        ],
        compiler_params=pltpu.CompilerParams(
            collective_id=0, has_side_effects=True, vmem_limit_bytes=16 * 1024 * 1024
        ),
    )(outgoing)


def round_up(n, tile):
    return -(-n // tile) * tile


def taps_of(cells, rows):
    parts = [cells[t * DILATION_STEP : t * DILATION_STEP + rows] for t in range(KERNEL_TAPS)]
    return jnp.concatenate(parts, axis=1)


def attend(query, new_key, new_value, cache_key, cache_value, cache_len):
    count, heads, positions, depth = cache_key.shape
    scale = 1.0 / jnp.sqrt(jnp.float32(depth))
    queries = query.reshape(count, heads, depth)
    fresh_key = new_key.reshape(count, heads, depth)
    fresh_value = new_value.reshape(count, heads, depth)
    scores = (
        jnp.einsum("rhd,rhld->rhl", queries, cache_key, preferred_element_type=jnp.float32) * scale
    )
    own_score = (
        jnp.einsum("rhd,rhd->rh", queries, fresh_key, preferred_element_type=jnp.float32) * scale
    )
    valid = jnp.arange(positions, dtype=jnp.int32)[None, :] < cache_len[:, None]
    scores = jnp.where(valid[:, None, :], scores, -1e30)
    top = jnp.maximum(jnp.max(scores, axis=-1), own_score)
    expo = jnp.where(valid[:, None, :], jnp.exp(scores - top[..., None]), 0.0)
    own_expo = jnp.exp(own_score - top)
    total = jnp.sum(expo, axis=-1) + own_expo
    weights = (expo / total[..., None]).astype(jnp.bfloat16)
    own_weight = (own_expo / total).astype(jnp.bfloat16)
    mixed = jnp.einsum("rhl,rhld->rhd", weights, cache_value, preferred_element_type=jnp.float32)
    mixed = mixed + own_weight.astype(jnp.float32)[..., None] * fresh_value.astype(jnp.float32)
    return mixed.astype(jnp.bfloat16).reshape(count, heads * depth)


def body(
    query,
    new_key,
    new_value,
    cache_key,
    cache_value,
    cache_len,
    residual,
    out_weight,
    norm_gain,
    codec_weight,
    finished,
    owner,
    frames,
    snake_alpha,
    filter_weight,
    conv_bias,
):
    owners = lax.axis_size("dp")
    n_mp = lax.axis_size("mp")
    core = lax.axis_index("mp")
    tally, own = frames.shape
    span = KERNEL_TAPS // 2 * DILATION_STEP
    late = owners * CAP
    near = -(-span // CAP)
    front = round_up(late + span, ROW_TILE)
    back = round_up(span, ROW_TILE)

    wide_frames = frames.astype(jnp.float32)
    alpha_all = gather_mp(snake_alpha, 0)
    early = gather_mp(snake(wide_frames, snake_alpha), 1)
    head_frames = gather_mp(frames[:late], 1)
    before = lax.ppermute(early[tally - span :], "dp", [(i, i + 1) for i in range(owners - 1)])
    after_frames = lax.ppermute(
        head_frames[: near * CAP], "dp", [(i + 1, i) for i in range(owners - 1)]
    )
    middle = tally - front - back
    main = wide_frames[front : tally - back] + conv_bias
    for t in range(KERNEL_TAPS):
        start = front - span + t * DILATION_STEP
        main = main + jnp.dot(
            early[start : start + middle], filter_weight[t], preferred_element_type=jnp.float32
        )
    main = main.astype(jnp.bfloat16)

    attended = attend(query, new_key, new_value, cache_key, cache_value, cache_len)
    count = attended.shape[0]
    width = out_weight.shape[1]
    local_width = norm_gain.shape[0]
    residual_part = lax.dynamic_slice_in_dim(residual, core * local_width, local_width, 1)
    if n_mp == 2:
        tile = 1024
        theirs = columns_dot(
            attended, out_weight, (1 - core) * (local_width // tile), local_width, tile, jnp.bfloat16
        )
        arrived = swap(theirs)
        mine = columns_dot(
            attended, out_weight, core * (local_width // tile), local_width, tile, jnp.float32
        )
        projected = mine + arrived.astype(jnp.float32)
    else:
        term = jnp.dot(attended, out_weight, preferred_element_type=jnp.float32)
        projected = lax.psum_scatter(term, "mp", scatter_dimension=1, tiled=True)
    hidden = (residual_part.astype(jnp.float32) + projected).astype(jnp.bfloat16)
    wide = hidden.astype(jnp.float32)
    squares = jnp.sum(wide * wide, axis=-1)
    squares = squares + swap(squares) if n_mp == 2 else lax.psum(squares, "mp")
    meansq = squares / width
    normed = (wide * norm_gain.astype(jnp.float32)).astype(jnp.bfloat16)
    channels = codec_weight.shape[1]
    share = columns_dot(normed, codec_weight, 0, channels, 256, jnp.float32)
    share = (share * lax.rsqrt(meansq + 1e-05)[:, None]).astype(jnp.bfloat16)

    index = jnp.arange(count, dtype=jnp.int32)
    earlier = (
        (owner[:, None] == owner[None, :])
        & (finished[None, :] == 1)
        & (index[None, :] < index[:, None])
    )
    slot = jnp.sum(earlier.astype(jnp.int32), axis=1)
    target = owner * CAP + slot
    places = jnp.arange((owners + 1) * CAP, dtype=jnp.int32)
    onehot = ((places[:, None] == target[None, :]) & (finished[None, :] == 1)).astype(jnp.bfloat16)
    outgoing = jnp.dot(onehot, share, preferred_element_type=jnp.float32).astype(jnp.bfloat16)
    here, there = handoff(outgoing.reshape(owners + 1, CAP, channels), near)
    here = here.reshape(late, channels).astype(jnp.bfloat16).astype(jnp.float32)
    there = there.reshape(near * CAP, channels).astype(jnp.bfloat16).astype(jnp.float32)

    head_mix = head_frames.astype(jnp.float32) + here
    head_act = snake(head_mix, alpha_all)
    after = snake(after_frames.astype(jnp.float32) + there, alpha_all)[:span]
    cells_a = jnp.concatenate([before, head_act, early[late : front + span]], axis=0)
    cells_b = jnp.concatenate([early[tally - back - span :], after], axis=0)
    edges = jnp.concatenate([taps_of(cells_a, front), taps_of(cells_b, back)], axis=0)
    flat = filter_weight.reshape(KERNEL_TAPS * channels, own)
    own_mix = lax.dynamic_slice_in_dim(head_mix, core * own, own, 1)
    edge_mix = jnp.concatenate(
        [own_mix, wide_frames[late:front], wide_frames[tally - back :]], axis=0
    )
    edge = jnp.dot(edges, flat, preferred_element_type=jnp.float32) + edge_mix + conv_bias
    edge = edge.astype(jnp.bfloat16)
    audio = jnp.concatenate([edge[:front], main, edge[front:]], axis=0)
    return (hidden, audio)


def solution(mesh):
    placed = (
        P("dp", "mp"),
        P("dp", "mp"),
        P("dp", "mp"),
        P("dp", "mp", None, None),
        P("dp", "mp", None, None),
        P("dp"),
        P("dp", None),
        P("mp", None),
        P("mp"),
        P("mp", None),
        P("dp"),
        P("dp"),
        P("dp", "mp"),
        P("mp"),
        P(None, None, "mp"),
        P("mp"),
    )
    return jax.shard_map(
        body, mesh=mesh, in_specs=placed, out_specs=(P("dp", "mp"), P("dp", "mp")), check_vma=False
    )
```

time: 125 us -> 84.6 us (0.68)
  Pallas kernels: 0 us -> 36.8 us
  waiting for transfers between devices: 26.9 us -> 0.02 us
  matrix products: 43.2 us -> 19.3 us
  blocking collectives: 16.5 us -> 0 us
  between operations: 14.1 us -> 1.36 us
  other arithmetic: 10.9 us -> 13.1 us
    pallas_call x0 -> x4, Pallas kernels: none -> 36.8 us  [the longest x3 18.5 us: columns_dot(): pl.pallas_call(columns_kernel, out_shape=jax.ShapeDtypeStruct((rows, widt...]
    dot_general x10 -> x9, matrix products: 35.4 us -> 11.4 us  [the longest x7 9.84 us: body(): jnp.dot(early[start:start + middle], filter_weight[t], preferred_element_...]
    reduce_scatter x2 -> x0, waiting for transfers between devices: 18.4 us -> none  [the longest x1 12 us: body(): projected = lax.psum_scatter(term, 'mp', scatter_dimension=1, tiled=True)]
    all_to_all x1 -> x0, blocking collectives: 14.1 us -> none  [body(): lax.all_to_all(outgoing, 'dp', split_axis=0, concat_axis=0, tiled=True)]
    all_gather x1 -> x0, waiting for transfers between devices: 7.49 us -> none  [body(): channels = lax.all_gather(act, 'mp', axis=1, tiled=True)]
    select_n x0 -> x3, other arithmetic: none -> 3.31 us  [the longest x2 3.3 us: gather_mp(): jnp.where(first, x, other)]
    psum x1 -> x0, blocking collectives: 2.47 us -> none  [body(): squares = lax.psum(jnp.sum(wide * wide, axis=-1), 'mp')]
    unnamed x28 -> x39, local copies, waits for them, and re-layouts: 2.92 us -> 5.3 us
  transfers between devices with their start and end apart: 5 -> 7, of which waited for: 4 -> 0; matrix products, arithmetic and copies ran while one was open for 6% -> 24% of each run, Pallas kernels for 0% -> 44%
where the time goes in v1:
time: 84.6 us; the launch traced here: 83.9 us
  Pallas kernels  36.8 us (43%)
  matrix products  19.3 us (23%)
  other arithmetic  13.1 us (15%)
  local copies, waits for them, and re-layouts  6.9 us (8%)
  starting transfers between devices  6.5 us (8%)
  between operations  1.36 us (2%)
    pallas_call x3, Pallas kernels, columns_dot(): pl.pallas_call(columns_kernel, out_shape=jax.ShapeDtypeStruct((rows, widt...  18.5 us
    pallas_call x1, Pallas kernels, handoff(): pl.pallas_call(functools.partial(handoff_kernel, n_dp, n_mp, near), out_s...  18.2 us
    dot_general x7, matrix products, body(): jnp.dot(early[start:start + middle], filter_weight[t], preferred_element_...  9.84 us
    unnamed x39, local copies, waits for them, and re-layouts  5.3 us
    dot_general x1, matrix products, attend(): jnp.einsum('rhd,rhld->rhl', queries, cache_key, preferred_element_type=jn...  4.48 us
    convert_element_type x3, other arithmetic, snake(): return (mix + sin_squared(alpha * mix) / alpha).astype(jnp.bfloat16)  4.24 us
    ppermute x1, starting transfers between devices, body(): lax.ppermute(early[tally - span:], 'dp', [(i, i + 1) for i in range(owner...  3.44 us
    dot_general x1, matrix products, attend(): jnp.einsum('rhl,rhld->rhd', weights, cache_value, preferred_element_type=...  3.41 us
  transfers between devices with their start and end apart: 7, of which 0 were waited for; matrix products, arithmetic and copies ran while one was open for 24% of the time, Pallas kernels for 44%

profile of v1, /device:TPU:0, one launch (start us, length us, event | category | flops | bytes accessed | tf_op | source)
XLA Modules:
  0.0 83.9 jit_solution(2376928151737809769)
XLA Ops:
  0.6 0.6 collective-permute-start.5
  1.2 4.0 %fusion.7 = bf16[1024,512]{1,0:T(8,128)(2,1)} fusion(f32[512]{0:T(512)} %param.29, bf16[1024,512]{1,0:T(8,128)(2,1)} %param.28), kind=kLoop, calls=%fused_computation.24 | loop fusion | flops 13631488 | bytes 2099200 | tf_op jit(solution)/shard_map/convert_element_type | solution.py:41
  5.2 0.4 reshape.75
  5.7 4.5 %fusion.112 = f32[64,16,1,16]{3,2,1,0:T(1,128)S(1)} fusion(bf16[64,16,128,1]{2,3,1,0:T(2,128)(2,1)S(1)} %reshape.75, bf16[64,16,16,128]{3,2,1,0:T(8,128)(2,1)} %param.19), kind=kOutput, calls=%fused_computation.183 | convolution fusion | flops 4194304 | bytes 4521984 | tf_op jit(solution)/shard_map/rhd,rhld->rhl/dot_general | solution.py:221
  10.2 0.3 copy.20
  10.6 0.2 fusion.69
  11.1 0.5 copy.25
  11.8 3.4 %fusion.113 = f32[64,16,1,128]{3,2,1,0:T(1,128)S(1)} fusion(bf16[64,16,16,1]{2,3,1,0:T(2,128)(2,1)S(1)} %copy.25, bf16[64,16,16,128]{3,2,1,0:T(8,128)(2,1)} %param.20), kind=kOutput, calls=%fused_computation.184 | convolution fusion | flops 4194304 | bytes 4751360 | tf_op jit(solution)/shard_map/rhl,rhld->rhd/dot_general | solution.py:234
  15.6 7.7 %shard_map.168 = bf16[64,4096]{1,0:T(8,128)(2,1)S(1)} custom-call(s32[1]{0:T(128)} %bitcast.5.start_ref, bf16[64,2048]{1,0:T(8,128)(2,1)S(1)} %bitcast.65, bf16[2048,8192]{1,0:T(8,128)(2,1)} %w_ref.4), custom_call_target="tpu_custom_call" | custom-call | flops 1073741824 | bytes 16777216 | tf_op jit(solution)/shard_map/pallas_call | solution.py:53
  23.3 0.6 collective-permute-start
  24.2 7.7 %shard_map.167 = f32[64,4096]{1,0:T(8,128)S(1)} custom-call(s32[1]{0:T(128)} %bitcast.start_ref, bf16[64,2048]{1,0:T(8,128)(2,1)S(1)} %bitcast.66, bf16[2048,8192]{1,0:T(8,128)(2,1)} %w_ref.4), custom_call_target="tpu_custom_call" | custom-call | flops 1073741824 | bytes 16777216 | tf_op jit(solution)/shard_map/pallas_call | solution.py:53
  31.9 1.6 %convert_element_type.99 = f32[1024,512]{1,0:T(8,128)} convert(bf16[1024,512]{1,0:T(8,128)(2,1)S(1)} %copy-done.1) | non-fusion elementwise | flops 524288 | bytes 3145728 | tf_op jit(solution)/shard_map/convert_element_type | solution.py:267
  33.6 1.3 %collective-permute-start.6 = (bf16[12,1024]{1,0:T(8,128)(2,1)S(1)}, bf16[12,1024]{1,0:T(8,128)(2,1)S(1)}, u32[]{:S(2)}, u32[]{:S(2)}) collective-permute-start(bf16[12,1024]{1,0:T(8,128)(2,1)S(1)} %fusion.97), channel_id=1, source_target_pairs={{2,0},{4,2},{6,4},{8,6},{10,8},{12,10},{14,12},{16,14},{18,16},{20... | collective-permute-start | bytes 73736 | tf_op jit(solution)/shard_map/ppermute | solution.py:272
  34.9 1.5 %fusion.50 = (f32[64]{0:T(128)S(1)}, bf16[64,4096]{1,0:T(8,128)(2,1)S(1)}) fusion(f32[64,4096]{1,0:T(8,128)S(1)} %shard_map.167, bf16[64,4096]{1,0:T(8,128)(2,1)} %collective-permute-done, bf16[64,8192]{1,0:T(8,128)(2,1)} %param.22, s32[]{:T(128)S(6)} %select_n.49), kind=kLoop, calls=%fused_computation.60 | loop fusion | flops 2097088 | bytes 2621700 | tf_op jit(solution)/shard_map/reduce_sum | solution.py:304
  36.5 0.5 collective-permute-start.4
  37.1 3.4 %copy-done = bf16[4096,1024]{1,0:T(8,128)(2,1)S(1)} copy-done((bf16[4096,1024]{1,0:T(8,128)(2,1)S(1)}, bf16[4096,1024]{1,0:T(8,128)(2,1)}, u32[]{:S(2)}) %copy-start) | copy-done | bytes 8388632
  40.5 3.1 %shard_map.169 = f32[64,1024]{1,0:T(8,128)S(1)} custom-call(s32[1]{0:T(128)} %constant.43.clone.1.start_ref, bf16[64,4096]{1,0:T(8,128)(2,1)S(1)} %fusion.49.x_ref, bf16[4096,1024]{1,0:T(8,128)(2,1)S(1)} %copy-done), custom_call_target="tpu_custom_call" | custom-call | flops 536870912 | bytes 8388608 | tf_op jit(solution)/shard_map/pallas_call | solution.py:53
  43.7 0.2 convolution_convert_fusion
  44.0 18.2 %shard_map.170 = (f32[16,4,1024]{2,1,0:T(4,128)S(1)}, f32[3,4,1024]{2,1,0:T(4,128)S(1)}) custom-call(bf16[17,4,1024]{2,1,0:T(4,128)(2,1)S(1)} %reshape.63.out_ref), custom_call_target="tpu_custom_call" | custom-call | tf_op jit(solution)/shard_map/pallas_call | solution.py:183
  62.4 0.2 fusion.77
  62.8 3.3 %broadcast_select_fusion.1 = (bf16[1024,512]{1,0:T(8,128)(2,1)S(1)}, bf16[1024,512]{1,0:T(8,128)(2,1)S(1)}) fusion(bf16[1024,512]{1,0:T(8,128)(2,1)} %collective-permute-done.1, pred[]{:T(512)S(6)} %eq.17, f32[512]{0:T(512)S(1)} %copy-done.7, bf16[1024,512]{1,0:T(8,128)(2,1)S(1)} %copy-done.1), kind=kLoop, calls=%fused_computation.78 | loop fusion | flops 14680064 | bytes 4196353 | tf_op jit(solution)/shard_map/jit(_where)/select_n | solution.py:24
  66.1 2.5 %fusion.12 = f32[928,512]{1,0:T(8,128)S(1)} fusion(bf16[1024,512]{1,0:T(8,128)(2,1)S(1)} %get-tuple-element.13, bf16[1024,512]{1,0:T(8,128)(2,1)S(1)} %get-tuple-element.14, bf16[7,1024,512]{2,1,0:T(8,128)(2,1)} %param.30), kind=kOutput, calls=%fused_computation.28 | convolution fusion | flops 976879616 | bytes 5046272 | tf_op jit(solution)/shard_map/dot_general | solution.py:279
  68.7 1.1 %fusion.15 = f32[928,512]{1,0:T(8,128)S(1)} fusion(bf16[1024,512]{1,0:T(8,128)(2,1)S(1)} %get-tuple-element.13, bf16[1024,512]{1,0:T(8,128)(2,1)S(1)} %get-tuple-element.14, bf16[7,1024,512]{2,1,0:T(8,128)(2,1)S(1)} %bitcast.68), kind=kOutput, calls=%fused_computation.30 | convolution fusion | flops 976879616 | bytes 5046272 | tf_op jit(solution)/shard_map/dot_general | solution.py:279
  69.8 1.1 %fusion.18 = f32[928,512]{1,0:T(8,128)S(1)} fusion(bf16[1024,512]{1,0:T(8,128)(2,1)S(1)} %get-tuple-element.13, bf16[1024,512]{1,0:T(8,128)(2,1)S(1)} %get-tuple-element.14, bf16[7,1024,512]{2,1,0:T(8,128)(2,1)S(1)} %bitcast.68), kind=kOutput, calls=%fused_computation.32 | convolution fusion | flops 976879616 | bytes 5046272 | tf_op jit(solution)/shard_map/dot_general | solution.py:279
  71.0 1.1 %fusion.21 = f32[928,512]{1,0:T(8,128)S(1)} fusion(bf16[1024,512]{1,0:T(8,128)(2,1)S(1)} %get-tuple-element.13, bf16[1024,512]{1,0:T(8,128)(2,1)S(1)} %get-tuple-element.14, bf16[7,1024,512]{2,1,0:T(8,128)(2,1)S(1)} %bitcast.68), kind=kOutput, calls=%fused_computation.34 | convolution fusion | flops 976879616 | bytes 5046272 | tf_op jit(solution)/shard_map/dot_general | solution.py:279
  72.1 1.1 %fusion.24 = f32[928,512]{1,0:T(8,128)S(1)} fusion(bf16[1024,512]{1,0:T(8,128)(2,1)S(1)} %get-tuple-element.13, bf16[1024,512]{1,0:T(8,128)(2,1)S(1)} %get-tuple-element.14, bf16[7,1024,512]{2,1,0:T(8,128)(2,1)S(1)} %bitcast.68), kind=kOutput, calls=%fused_computation.36 | convolution fusion | flops 976879616 | bytes 5046272 | tf_op jit(solution)/shard_map/dot_general | solution.py:279
  73.3 1.1 %fusion.9 = f32[928,512]{1,0:T(8,128)S(1)} fusion(bf16[1024,512]{1,0:T(8,128)(2,1)S(1)} %get-tuple-element.13, bf16[1024,512]{1,0:T(8,128)(2,1)S(1)} %get-tuple-element.14, bf16[7,1024,512]{2,1,0:T(8,128)(2,1)S(1)} %bitcast.68), kind=kOutput, calls=%fused_computation.26 | convolution fusion | flops 976879616 | bytes 5046272 | tf_op jit(solution)/shard_map/dot_general | solution.py:279
  74.5 3.4 %collective-permute-start.2 = (bf16[9,1024]{1,0:T(8,128)(2,1)S(1)}, bf16[9,1024]{1,0:T(8,128)(2,1)S(1)}, u32[]{:S(2)}, u32[]{:S(2)}) collective-permute-start(bf16[9,1024]{1,0:T(8,128)(2,1)S(1)} %pad_maximum_fusion.10), channel_id=1, source_target_pairs={{0,2},{2,4},{4,6},{6,8},{8,10},{10,12},{12,14},{14,16},{16,18},{18... | collective-permute-start | bytes 55304 | tf_op jit(solution)/shard_map/ppermute | solution.py:271
  78.1 1.5 %copy-done.2 = f32[1024,512]{1,0:T(8,128)S(1)} copy-done((f32[1024,512]{1,0:T(8,128)S(1)}, f32[1024,512]{1,0:T(8,128)}, u32[]{:S(2)}) %copy-start.2) | copy-done | bytes 2097176
  79.6 1.6 %fusion.35 = bf16[928,512]{1,0:T(8,128)(2,1)S(1)} fusion(f32[928,512]{1,0:T(8,128)S(1)} %fusion.9, f32[928,512]{1,0:T(8,128)S(1)} %fusion.24, f32[928,512]{1,0:T(8,128)S(1)} %fusion.21, f32[928,512]{1,0:T(8,128)S(1)} %fusion.18, f32[928,512]{1,0:T(8,128)S(1)} %fusion.15, f32[928,512]{1,0:T(8,128)S(1)} %fusion.12, f32[1024,512]{1,0:T(8,128)S(1)} %copy-done.2, ...), kind=kOutput, calls=%fused_computation.48 | convolution fusion | flops 981155840 | bytes 17401856 | tf_op jit(solution)/shard_map/dot_general | solution.py:279
  81.5 1.3 %fusion.46 = bf16[96,512]{1,0:T(8,128)(2,1)S(1)} fusion(bf16[7168,512]{1,0:T(8,128)(2,1)S(1)} %bitcast.69, bf16[16,7168]{1,0:T(8,128)(2,1)S(1)} %slice_dynamic-update-slice_fusion.3, bf16[80,7168]{1,0:T(8,128)(2,1)S(1)} %fusion.84, f32[16,512]{1,0:T(8,128)S(1)} %get-tuple-element.18, f32[16,512]{1,0:T(8,128)S(1)} %get-tuple-element.17, ...), kind=kOutput, calls=%fused_computation.58 | convolution fusion | flops 707641344 | bytes 9013248 | tf_op jit(solution)/shard_map/dot_general | solution.py:338
  82.9 1.0 %pad_maximum_fusion.2 = bf16[1024,512]{1,0:T(8,128)(2,1)} fusion(bf16[16,512]{1,0:T(8,128)(2,1)S(1)} %slice.197, bf16[928,512]{1,0:T(8,128)(2,1)S(1)} %fusion.35, bf16[80,512]{1,0:T(8,128)(2,1)S(1)} %slice.183), kind=kLoop, calls=%fused_computation.61 | loop fusion | flops 3145728 | bytes 2097152 | tf_op jit(solution)/shard_map/concatenate | solution.py:340
  (92 shorter events, 2.1 us)
Async XLA Ops:
  0.6 4.6 %copy-start.4 = (bf16[64,2048]{1,0:T(8,128)(2,1)S(1)}, bf16[64,2048]{1,0:T(8,128)(2,1)}, u32[]{:S(2)}) copy-start(bf16[64,2048]{1,0:T(8,128)(2,1)} %param.16) | copy-start | bytes 786436
  0.6 32.9 %collective-permute-start.5 = (f32[512]{0:T(512)}, f32[512]{0:T(512)S(1)}, u32[]{:S(2)}, u32[]{:S(2)}) collective-permute-start(f32[512]{0:T(512)} %param.29), channel_id=1, source_target_pairs={{0,1},{1,0},{2,3},{3,2},{4,5},{5,4},{6,7},{7,6},{8,9},{9,8},{10,11... | collective-permute-start | bytes 6152 | tf_op jit(solution)/shard_map/ppermute | solution.py:16
  5.2 57.6 %collective-permute-start.1 = (bf16[1024,512]{1,0:T(8,128)(2,1)}, bf16[1024,512]{1,0:T(8,128)(2,1)}, u32[]{:S(2)}, u32[]{:S(2)}) collective-permute-start(bf16[1024,512]{1,0:T(8,128)(2,1)} %fusion.7), channel_id=1, source_target_pairs={{0,1},{1,0},{2,3},{3,2},{4,5},{5,4},{6,7},{7,6},{8,9},{9,8},{10,11... | collective-permute-start | bytes 3145736 | tf_op jit(solution)/shard_map/ppermute | solution.py:16
  5.6 4.8 %copy-start.11 = (s32[64]{0:T(128)S(1)}, s32[64]{0:T(128)}, u32[]{:S(2)}) copy-start(s32[64]{0:T(128)} %param.21) | copy-start | bytes 772
  5.6 4.9 %copy-start.6 = (bf16[64,2048]{1,0:T(8,128)(2,1)S(1)}, bf16[64,2048]{1,0:T(8,128)(2,1)}, u32[]{:S(2)}) copy-start(bf16[64,2048]{1,0:T(8,128)(2,1)} %param.17) | copy-start | bytes 786436
  10.1 1.5 %copy-start.5 = (bf16[64,2048]{1,0:T(8,128)(2,1)S(1)}, bf16[64,2048]{1,0:T(8,128)(2,1)}, u32[]{:S(2)}) copy-start(bf16[64,2048]{1,0:T(8,128)(2,1)} %param.18) | copy-start | bytes 786436
  15.5 8.3 %copy-start.1 = (bf16[1024,512]{1,0:T(8,128)(2,1)S(1)}, bf16[1024,512]{1,0:T(8,128)(2,1)}, u32[]{:S(2)}) copy-start(bf16[1024,512]{1,0:T(8,128)(2,1)} %param.28) | copy-start | bytes 3145732
  15.5 8.4 %copy-start.12 = (s32[64]{0:T(128)S(1)}, s32[64]{0:T(128)}, u32[]{:S(2)}) copy-start(s32[64]{0:T(128)} %param.26) | copy-start | bytes 772
  15.6 8.4 %copy-start.10 = (s32[64]{0:T(128)S(1)}, s32[64]{0:T(128)}, u32[]{:S(2)}) copy-start(s32[64]{0:T(128)} %param.27) | copy-start | bytes 772
  23.3 11.6 %collective-permute-start = (bf16[64,4096]{1,0:T(8,128)(2,1)S(1)}, bf16[64,4096]{1,0:T(8,128)(2,1)}, u32[]{:S(2)}, u32[]{:S(2)}) collective-permute-start(bf16[64,4096]{1,0:T(8,128)(2,1)S(1)} %shard_map.168), channel_id=1, source_target_pairs={{0,1},{1,0},{2,3},{3,2},{4,5},{5,4},{6,7},{7,6},{8,9},{9,8},{10,11... | collective-permute-start | bytes 1572872 | tf_op jit(solution)/shard_map/ppermute | solution.py:16
  23.9 9.7 %collective-permute-start.3 = (bf16[64,512]{1,0:T(8,128)(2,1)S(1)}, bf16[64,512]{1,0:T(8,128)(2,1)S(1)}, u32[]{:S(2)}, u32[]{:S(2)}) collective-permute-start(bf16[64,512]{1,0:T(8,128)(2,1)S(1)} %slice.126), channel_id=1, source_target_pairs={{0,1},{1,0},{2,3},{3,2},{4,5},{5,4},{6,7},{7,6},{8,9},{9,8},{10,11... | collective-permute-start | bytes 196616 | tf_op jit(solution)/shard_map/ppermute | solution.py:16
  31.9 1.7 %copy-start.9 = (bf16[4096]{0:T(1024)(128)(2,1)S(1)}, bf16[4096]{0:T(1024)(128)(2,1)}, u32[]{:S(2)}) copy-start(bf16[4096]{0:T(1024)(128)(2,1)} %param.24) | copy-start | bytes 24580
  31.9 1.7 %copy-start.7 = (f32[512]{0:T(512)S(1)}, f32[512]{0:T(512)}, u32[]{:S(2)}) copy-start(f32[512]{0:T(512)} %param.29) | copy-start | bytes 6148
  33.6 29.1 %collective-permute-start.6 = (bf16[12,1024]{1,0:T(8,128)(2,1)S(1)}, bf16[12,1024]{1,0:T(8,128)(2,1)S(1)}, u32[]{:S(2)}, u32[]{:S(2)}) collective-permute-start(bf16[12,1024]{1,0:T(8,128)(2,1)S(1)} %fusion.97), channel_id=1, source_target_pairs={{2,0},{4,2},{6,4},{8,6},{10,8},{12,10},{14,12},{16,14},{18,16},{20... | collective-permute-start | bytes 73736 | tf_op jit(solution)/shard_map/ppermute | solution.py:272
  36.5 7.2 %copy-start.3 = (bf16[64,4096]{1,0:T(8,128)(2,1)}, bf16[64,4096]{1,0:T(8,128)(2,1)S(1)}, u32[]{:S(2)}) copy-start(bf16[64,4096]{1,0:T(8,128)(2,1)S(1)} %get-tuple-element.12) | copy-start | bytes 1572868
  36.5 7.2 %collective-permute-start.4 = (f32[64]{0:T(128)S(1)}, f32[64]{0:T(128)S(1)}, u32[]{:S(2)}, u32[]{:S(2)}) collective-permute-start(f32[64]{0:T(128)S(1)} %get-tuple-element.11), channel_id=1, source_target_pairs={{0,1},{1,0},{2,3},{3,2},{4,5},{5,4},{6,7},{7,6},{8,9},{9,8},{10,11... | collective-permute-start | bytes 776 | tf_op jit(solution)/shard_map/ppermute | solution.py:16
  37.1 3.4 %copy-start = (bf16[4096,1024]{1,0:T(8,128)(2,1)S(1)}, bf16[4096,1024]{1,0:T(8,128)(2,1)}, u32[]{:S(2)}) copy-start(bf16[4096,1024]{1,0:T(8,128)(2,1)} %w_ref.5) | copy-start | bytes 25165828
  62.8 5.8 %slice-start = ((s8[7340032]{0:T(1024)(128)(4,1)}), s8[4194304]{0:T(1024)(128)(4,1)S(1)}, s32[]{:S(2)}) async-start(s8[7340032]{0:T(1024)(128)(4,1)} %bitcast.67), calls=%async_computation | async-start | bytes 8388608
  66.1 2.5 %slice-start.1 = ((s8[7340032]{0:T(1024)(128)(4,1)}), s8[3145728]{0:T(1024)(128)(4,1)S(1)}, s32[]{:S(2)}) async-start(s8[7340032]{0:T(1024)(128)(4,1)} %bitcast.67), calls=%async_computation.1 | async-start | bytes 6291456
  74.5 6.7 %collective-permute-start.2 = (bf16[9,1024]{1,0:T(8,128)(2,1)S(1)}, bf16[9,1024]{1,0:T(8,128)(2,1)S(1)}, u32[]{:S(2)}, u32[]{:S(2)}) collective-permute-start(bf16[9,1024]{1,0:T(8,128)(2,1)S(1)} %pad_maximum_fusion.10), channel_id=1, source_target_pairs={{0,2},{2,4},{4,6},{6,8},{8,10},{10,12},{12,14},{14,16},{16,18},{18... | collective-permute-start | bytes 55304 | tf_op jit(solution)/shard_map/ppermute | solution.py:271
  78.0 1.6 %copy-start.2 = (f32[1024,512]{1,0:T(8,128)S(1)}, f32[1024,512]{1,0:T(8,128)}, u32[]{:S(2)}) copy-start(f32[1024,512]{1,0:T(8,128)} %convert_element_type.99) | copy-start | bytes 6291460
  78.0 1.6 %copy-start.8 = (f32[512]{0:T(512)S(1)}, f32[512]{0:T(512)}, u32[]{:S(2)}) copy-start(f32[512]{0:T(512)} %param.31) | copy-start | bytes 6148

commit v2 on v1

--- a/solution.py
+++ b/solution.py
@@ -38,7 +38,7 @@
 
 
 def snake(mix, alpha):
-    return (mix + sin_squared(alpha * mix) / alpha).astype(jnp.bfloat16)
+    return (mix + sin_squared(alpha * mix) * (1.0 / alpha)).astype(jnp.bfloat16)
 
 
 def columns_kernel(start_ref, x_ref, w_ref, o_ref):
@@ -62,7 +62,7 @@
             ],
             out_specs=pl.BlockSpec((rows, tile), lambda j, s: (0, j)),
         ),
-        compiler_params=pltpu.CompilerParams(vmem_limit_bytes=28 * 1024 * 1024),
+        compiler_params=pltpu.CompilerParams(vmem_limit_bytes=60 * 1024 * 1024),
         cost_estimate=pl.CostEstimate(
             flops=2 * rows * depth * width, bytes_accessed=2 * depth * width, transcendentals=0
         ),
@@ -70,131 +70,147 @@
 
 
 def handoff_kernel(
-    n_dp, n_mp, near, out_ref, a_ref, b_ref, land_a, land_b, send_a, recv_a, send_b, recv_b
+    n_dp, n_mp, near, out_ref, a_ref, b_ref, land_a, land_b,
+    own_sem, send_a, recv_a, send_b, recv_b, share_send, share_recv,
 ):
     dp = lax.axis_index("dp")
     mp = lax.axis_index("mp")
-    count = n_dp * n_mp
-    me = dp * n_mp + mp
     barrier = pltpu.get_barrier_semaphore()
-
-    def place(step):
-        peer = lax.rem(me + step, count)
-        return peer, peer // n_mp, lax.rem(peer, n_mp)
+    mesh_id = pl.DeviceIdType.MESH
+    width = out_ref.shape[2]
+
+    def peer_of(step):
+        return lax.rem(dp + step, n_dp)
+
+    def core_of(step):
+        return lax.rem(mp + step, n_mp)
 
     def greet(step, carry):
-        _, pd, pm = place(step)
-        pl.semaphore_signal(
-            barrier, inc=1, device_id=(pd, pm), device_id_type=pl.DeviceIdType.MESH
-        )
-        return carry
-
-    lax.fori_loop(1, count, greet, 0)
-    pl.semaphore_wait(barrier, count - 1)
-
-    def copy_a(pd, pm, send, recv):
+        pl.semaphore_signal(barrier, inc=1, device_id=(peer_of(step), mp), device_id_type=mesh_id)
+        return carry
+
+    lax.fori_loop(1, n_dp, greet, 0)
+    for c in range(1, n_mp):
+        pl.semaphore_signal(barrier, inc=1, device_id=(dp, core_of(c)), device_id_type=mesh_id)
+    pl.semaphore_wait(barrier, n_dp - 1 + n_mp - 1)
+
+    def copy_a(pd, recv):
         return pltpu.make_async_remote_copy(
             src_ref=out_ref.at[pd],
-            dst_ref=land_a.at[me],
-            send_sem=send_a.at[send],
+            dst_ref=land_a.at[mp, dp],
+            send_sem=send_a.at[pd],
             recv_sem=recv_a.at[recv],
-            device_id=(pd, pm),
-            device_id_type=pl.DeviceIdType.MESH,
-        )
-
-    def copy_b(slot, pd, pm, send, recv):
+            device_id=(pd, mp),
+            device_id_type=mesh_id,
+        )
+
+    def copy_b(slot, pd, recv):
         return pltpu.make_async_remote_copy(
             src_ref=out_ref.at[pd + 1],
-            dst_ref=land_b.at[slot],
-            send_sem=send_b.at[send],
+            dst_ref=land_b.at[mp, slot],
+            send_sem=send_b.at[pd],
             recv_sem=recv_b.at[recv],
-            device_id=(pd, pm),
-            device_id_type=pl.DeviceIdType.MESH,
+            device_id=(pd, mp),
+            device_id_type=mesh_id,
+        )
+
+    def share(ref, kind, c, core, slot):
+        return pltpu.make_async_remote_copy(
+            src_ref=ref.at[mp],
+            dst_ref=ref.at[slot],
+            send_sem=share_send.at[kind, c],
+            recv_sem=share_recv.at[kind, c],
+            device_id=(dp, core),
+            device_id_type=mesh_id,
         )
 
     def send(step, carry):
-        peer, pd, pm = place(step)
-        copy_a(pd, pm, peer, me).start()
+        pd = peer_of(step)
+        copy_a(pd, dp).start()
         return carry
 
     def send_near(step, carry):
-        peer, pd, pm = place(step)
-        copy_b(me, pd, pm, peer, me).start()
-        return carry
+        copy_b(dp, peer_of(step), dp).start()
+        return carry
+
+    lax.fori_loop(1, n_dp, send, 0)
+    own_a = pltpu.make_async_copy(out_ref.at[dp], land_a.at[mp, dp], own_sem.at[0])
+    own_a.start()
 
     @pl.when(dp < near)
     def _():
-        lax.fori_loop(1, count, send_near, 0)
-
-    lax.fori_loop(1, count, send, 0)
-    land_a[me] = out_ref[dp]
+        lax.fori_loop(1, n_dp, send_near, 0)
+        own_b = pltpu.make_async_copy(out_ref.at[dp + 1], land_b.at[mp, dp], own_sem.at[1])
+        own_b.start()
+        own_b.wait()
+
+    own_a.wait()
+
+    def finish(step, carry):
+        pd = peer_of(step)
+        copy_a(pd, pd).wait_recv()
+        return carry
+
+    def leave(step, carry):
+        copy_a(peer_of(step), dp).wait_send()
+        return carry
+
+    def leave_near(step, carry):
+        copy_b(dp, peer_of(step), dp).wait_send()
+        return carry
+
+    def take_near(sender, carry):
+        @pl.when(sender != dp)
+        def _():
+            copy_b(sender, 0, sender).wait_recv()
+
+        return carry
+
+    lax.fori_loop(1, n_dp, finish, 0)
+    for c in range(1, n_mp):
+        share(land_a, 0, c, core_of(c), mp).start()
+    lax.fori_loop(0, near, take_near, 0)
+    for c in range(1, n_mp):
+        share(land_b, 1, c, core_of(c), mp).start()
+    lax.fori_loop(1, n_dp, leave, 0)
 
     @pl.when(dp < near)
     def _():
-        land_b[me] = out_ref[dp + 1]
-
-    def finish(step, carry):
-        peer, pd, pm = place(step)
-        copy = copy_a(pd, pm, peer, peer)
-        copy.wait_recv()
-        copy.wait_send()
-        return carry
-
-    def finish_near(step, carry):
-        peer, pd, pm = place(step)
-        copy_b(me, pd, pm, peer, me).wait_send()
-        return carry
-
-    def take_near(sender, carry):
-        @pl.when(sender != me)
-        def _():
-            copy_b(sender, 0, 0, sender, sender).wait_recv()
-
-        return carry
-
-    lax.fori_loop(1, count, finish, 0)
-
-    @pl.when(dp < near)
-    def _():
-        lax.fori_loop(1, count, finish_near, 0)
-
-    lax.fori_loop(0, near * n_mp, take_near, 0)
-
-    def total_of(land, first):
-        total = land[first].astype(jnp.float32)
-        for m in range(1, n_mp):
-            total = total + land[first + m].astype(jnp.float32)
-        return total
-
-    def put(d, carry):
-        a_ref[d] = total_of(land_a, d * n_mp)
-        return carry
-
-    lax.fori_loop(0, n_dp, put, 0)
-    for d in range(near):
-        b_ref[d] = total_of(land_b, d * n_mp)
+        lax.fori_loop(1, n_dp, leave_near, 0)
+
+    for kind, ref in ((0, land_a), (1, land_b)):
+        for c in range(1, n_mp):
+            copy = share(ref, kind, c, core_of(c), core_of(n_mp - c))
+            copy.wait_send()
+            copy.wait_recv()
+    for m in range(n_mp):
+        a_ref[:, :, m * width : (m + 1) * width] = land_a[m].astype(jnp.float32)
+        b_ref[:, :, m * width : (m + 1) * width] = land_b[m].astype(jnp.float32)
 
 
 def handoff(outgoing, near):
     n_dp, n_mp = lax.axis_size("dp"), lax.axis_size("mp")
-    count = n_dp * n_mp
     _, cap, width = outgoing.shape
     vmem = pl.BlockSpec(memory_space=pltpu.VMEM)
+    dma = pltpu.SemaphoreType.DMA
     return pl.pallas_call(
         functools.partial(handoff_kernel, n_dp, n_mp, near),
         out_shape=(
-            jax.ShapeDtypeStruct((n_dp, cap, width), jnp.float32),
-            jax.ShapeDtypeStruct((near, cap, width), jnp.float32),
+            jax.ShapeDtypeStruct((n_dp, cap, n_mp * width), jnp.float32),
+            jax.ShapeDtypeStruct((near, cap, n_mp * width), jnp.float32),
         ),
         in_specs=[vmem],
         out_specs=(vmem, vmem),
         scratch_shapes=[
-            pltpu.VMEM((count, cap, width), jnp.bfloat16),
-            pltpu.VMEM((near * n_mp, cap, width), jnp.bfloat16),
-            pltpu.SemaphoreType.DMA((count,)),
-            pltpu.SemaphoreType.DMA((count,)),
-            pltpu.SemaphoreType.DMA((count,)),
-            pltpu.SemaphoreType.DMA((near * n_mp,)),
+            pltpu.VMEM((n_mp, n_dp, cap, width), jnp.bfloat16),
+            pltpu.VMEM((n_mp, near, cap, width), jnp.bfloat16),
+            dma((2,)),
+            dma((n_dp,)),
+            dma((n_dp,)),
+            dma((n_dp,)),
+            dma((near,)),
+            dma((2, n_mp)),
+            dma((2, n_mp)),
         ],
         compiler_params=pltpu.CompilerParams(
             collective_id=0, has_side_effects=True, vmem_limit_bytes=16 * 1024 * 1024
@@ -267,8 +283,9 @@
     wide_frames = frames.astype(jnp.float32)
     alpha_all = gather_mp(snake_alpha, 0)
     early = gather_mp(snake(wide_frames, snake_alpha), 1)
-    head_frames = gather_mp(frames[:late], 1)
-    before = lax.ppermute(early[tally - span :], "dp", [(i, i + 1) for i in range(owners - 1)])
+    ends = gather_mp(jnp.concatenate([frames[:late], frames[tally - back :]], axis=0), 1)
+    head_frames = ends[:late]
+    before = lax.ppermute(ends[late:], "dp", [(i, i + 1) for i in range(owners - 1)])
     after_frames = lax.ppermute(
         head_frames[: near * CAP], "dp", [(i + 1, i) for i in range(owners - 1)]
     )
@@ -307,7 +324,13 @@
     normed = (wide * norm_gain.astype(jnp.float32)).astype(jnp.bfloat16)
     channels = codec_weight.shape[1]
     share = columns_dot(normed, codec_weight, 0, channels, 256, jnp.float32)
-    share = (share * lax.rsqrt(meansq + 1e-05)[:, None]).astype(jnp.bfloat16)
+    if n_mp == 2:
+        given = lax.dynamic_slice_in_dim(share, (1 - core) * own, own, 1).astype(jnp.bfloat16)
+        kept = lax.dynamic_slice_in_dim(share, core * own, own, 1)
+        latent = kept + swap(given).astype(jnp.float32)
+    else:
+        latent = lax.psum_scatter(share, "mp", scatter_dimension=1, tiled=True)
+    latent = (latent * lax.rsqrt(meansq + 1e-05)[:, None]).astype(jnp.bfloat16)
 
     index = jnp.arange(count, dtype=jnp.int32)
     earlier = (
@@ -319,14 +342,15 @@
     target = owner * CAP + slot
     places = jnp.arange((owners + 1) * CAP, dtype=jnp.int32)
     onehot = ((places[:, None] == target[None, :]) & (finished[None, :] == 1)).astype(jnp.bfloat16)
-    outgoing = jnp.dot(onehot, share, preferred_element_type=jnp.float32).astype(jnp.bfloat16)
-    here, there = handoff(outgoing.reshape(owners + 1, CAP, channels), near)
-    here = here.reshape(late, channels).astype(jnp.bfloat16).astype(jnp.float32)
-    there = there.reshape(near * CAP, channels).astype(jnp.bfloat16).astype(jnp.float32)
+    outgoing = jnp.dot(onehot, latent, preferred_element_type=jnp.float32).astype(jnp.bfloat16)
+    here, there = handoff(outgoing.reshape(owners + 1, CAP, own), near)
+    here = here.reshape(late, channels)
+    there = there.reshape(near * CAP, channels)
 
     head_mix = head_frames.astype(jnp.float32) + here
     head_act = snake(head_mix, alpha_all)
     after = snake(after_frames.astype(jnp.float32) + there, alpha_all)[:span]
+    before = snake(before.astype(jnp.float32), alpha_all)[back - span :]
     cells_a = jnp.concatenate([before, head_act, early[late : front + span]], axis=0)
     cells_b = jnp.concatenate([early[tally - back - span :], after], axis=0)
     edges = jnp.concatenate([taps_of(cells_a, front), taps_of(cells_b, back)], axis=0)

time: 84.6 us -> 90.2 us (1.066)
  other arithmetic: 13.1 us -> 16 us
  Pallas kernels: 36.8 us -> 35.2 us
  local copies, waits for them, and re-layouts: 6.9 us -> 8.27 us
  waiting for transfers between devices: 0.02 us -> 1.23 us
  starting transfers between devices: 6.5 us -> 7.45 us
    pallas_call x1, Pallas kernels: 18.2 us -> 12.4 us  [handoff(): pl.pallas_call(functools.partial(handoff_kernel, n_dp, n_mp, near), out_s...]
    pallas_call x3, Pallas kernels: 18.5 us -> 22.8 us  [columns_dot(): pl.pallas_call(columns_kernel, out_shape=jax.ShapeDtypeStruct((rows, widt...]
    unnamed x39 -> x47, local copies, waits for them, and re-layouts: 5.3 us -> 2.92 us
    ppermute x1, starting transfers between devices: 3.44 us -> 4.86 us  [body(): lax.ppermute(ends[late:], 'dp', [(i, i + 1) for i in range(owners - 1)])]
    reshape x1 -> x3, local copies, waits for them, and re-layouts: 0.06 us -> 1.47 us  [the longest x1 0.79 us: body(): here = here.reshape(late, channels)]
    convert_element_type x1, other arithmetic: 1.63 us -> 0.27 us  [body(): wide_frames = frames.astype(jnp.float32)]
    convert_element_type x5 -> x4, other arithmetic: 4.26 us -> 5.56 us  [the longest x3 4.93 us: snake(): return (mix + sin_squared(alpha * mix) * (1.0 / alpha)).astype(jnp.bfloat16)]
    ppermute x5 -> x6, waiting for transfers between devices: 0.01 us -> 1.23 us  [swap(): return lax.ppermute(x, 'mp', [(0, 1), (1, 0)])]
  transfers between devices with their start and end apart: 7 -> 8, of which waited for: 0 -> 1; matrix products, arithmetic and copies ran while one was open for 24% -> 30% of each run, Pallas kernels for 44% -> 39%
where the time goes in v2:
time: 90.2 us; the launch traced here: 89.6 us
  Pallas kernels  35.2 us (39%)
  matrix products  20.2 us (22%)
  other arithmetic  16 us (18%)
  local copies, waits for them, and re-layouts  8.27 us (9%)
  starting transfers between devices  7.45 us (8%)
  between operations  1.25 us (1%)
  waiting for transfers between devices  1.23 us (1%)
    pallas_call x3, Pallas kernels, columns_dot(): pl.pallas_call(columns_kernel, out_shape=jax.ShapeDtypeStruct((rows, widt...  22.8 us
    pallas_call x1, Pallas kernels, handoff(): pl.pallas_call(functools.partial(handoff_kernel, n_dp, n_mp, near), out_s...  12.4 us
    dot_general x7, matrix products, body(): jnp.dot(early[start:start + middle], filter_weight[t], preferred_element_...  9.92 us
    convert_element_type x3, other arithmetic, snake(): return (mix + sin_squared(alpha * mix) * (1.0 / alpha)).astype(jnp.bfloat16)  4.93 us
    ppermute x1, starting transfers between devices, body(): lax.ppermute(ends[late:], 'dp', [(i, i + 1) for i in range(owners - 1)])  4.86 us
    dot_general x1, matrix products, attend(): jnp.einsum('rhd,rhld->rhl', queries, cache_key, preferred_element_type=jn...  4.49 us
    select_n x3, other arithmetic, gather_mp(): jnp.where(first, x, other)  3.48 us
    dot_general x1, matrix products, attend(): jnp.einsum('rhl,rhld->rhd', weights, cache_value, preferred_element_type=...  3.41 us
  transfers between devices with their start and end apart: 8, of which 1 were waited for; matrix products, arithmetic and copies ran while one was open for 30% of the time, Pallas kernels for 39%

profile of v2, /device:TPU:0, one launch (start us, length us, event | category | flops | bytes accessed | tf_op | source)
XLA Modules:
  0.0 89.6 jit_solution(11957959215288723351)
XLA Ops:
  1.2 1.3 %reshape.89 = bf16[64,16,128,1]{2,3,1,0:T(2,128)(2,1)S(1)} reshape(bf16[64,2048]{1,0:T(8,128)(2,1)} %param.16) | data formatting | bytes 524288 | tf_op jit(solution)/shard_map/reshape | solution.py:233
  2.6 4.5 %fusion.117 = f32[64,16,1,16]{3,2,1,0:T(1,128)S(1)} fusion(bf16[64,16,128,1]{2,3,1,0:T(2,128)(2,1)S(1)} %reshape.89, bf16[64,16,16,128]{3,2,1,0:T(8,128)(2,1)} %param.19), kind=kOutput, calls=%fused_computation.193 | convolution fusion | flops 4194304 | bytes 4521984 | tf_op jit(solution)/shard_map/rhd,rhld->rhl/dot_general | solution.py:237
  8.7 3.4 %fusion.118 = f32[64,16,1,128]{3,2,1,0:T(1,128)S(1)} fusion(bf16[64,16,16,1]{2,3,1,0:T(2,128)(2,1)S(1)} %copy.25, bf16[64,16,16,128]{3,2,1,0:T(8,128)(2,1)} %param.20), kind=kOutput, calls=%fused_computation.194 | convolution fusion | flops 4194304 | bytes 4751360 | tf_op jit(solution)/shard_map/rhl,rhld->rhd/dot_general | solution.py:250
  12.4 0.8 copy.33
  13.2 8.5 %shard_map.168 = bf16[64,4096]{1,0:T(8,128)(2,1)} custom-call(s32[1]{0:T(128)} %bitcast.5.start_ref, bf16[64,2048]{1,0:T(8,128)(2,1)} %bitcast.68, bf16[2048,8192]{1,0:T(8,128)(2,1)} %w_ref.4), custom_call_target="tpu_custom_call" | custom-call | flops 1073741824 | bytes 16777216 | tf_op jit(solution)/shard_map/pallas_call | solution.py:53
  23.1 8.5 %shard_map.167 = f32[64,4096]{1,0:T(8,128)} custom-call(s32[1]{0:T(128)} %bitcast.start_ref, bf16[64,2048]{1,0:T(8,128)(2,1)} %bitcast.69, bf16[2048,8192]{1,0:T(8,128)(2,1)} %w_ref.4), custom_call_target="tpu_custom_call" | custom-call | flops 1073741824 | bytes 16777216 | tf_op jit(solution)/shard_map/pallas_call | solution.py:53
  32.3 2.8 %fusion.3 = bf16[1024,512]{1,0:T(8,128)(2,1)} fusion(f32[512]{0:T(512)S(1)} %get-tuple-element.29, f32[512]{0:T(512)S(1)} %copy-done.11, bf16[1024,512]{1,0:T(8,128)(2,1)S(1)} %copy-done), kind=kLoop, calls=%fused_computation.16 | loop fusion | flops 13631488 | bytes 2101248 | tf_op jit(solution)/shard_map/convert_element_type | solution.py:41
  35.2 4.9 %collective-permute-start.2 = (bf16[16,1024]{1,0:T(8,128)(2,1)S(1)}, bf16[16,1024]{1,0:T(8,128)(2,1)S(1)}, u32[]{:S(2)}, u32[]{:S(2)}) collective-permute-start(bf16[16,1024]{1,0:T(8,128)(2,1)S(1)} %pad_maximum_fusion.11), channel_id=1, source_target_pairs={{0,2},{2,4},{4,6},{6,8},{8,10},{10,12},{12,14},{14,16},{16,18},{18... | collective-permute-start | bytes 98312 | tf_op jit(solution)/shard_map/ppermute | solution.py:288
  40.7 1.3 %collective-permute-start.7 = (bf16[12,1024]{1,0:T(8,128)(2,1)}, bf16[12,1024]{1,0:T(8,128)(2,1)}, u32[]{:S(2)}, u32[]{:S(2)}) collective-permute-start(bf16[12,1024]{1,0:T(8,128)(2,1)} %pad_maximum_fusion.10), channel_id=1, source_target_pairs={{2,0},{4,2},{6,4},{8,6},{10,8},{12,10},{14,12},{16,14},{18,16},{20... | collective-permute-start | bytes 73736 | tf_op jit(solution)/shard_map/ppermute | solution.py:289
  42.7 0.7 multiply_subtract_fusion.1
  43.4 1.4 %fusion.50 = (f32[64]{0:T(128)S(1)}, bf16[64,4096]{1,0:T(8,128)(2,1)S(1)}) fusion(f32[64,4096]{1,0:T(8,128)S(1)} %copy-done.1, bf16[64,4096]{1,0:T(8,128)(2,1)} %collective-permute-done, bf16[64,8192]{1,0:T(8,128)(2,1)S(1)} %copy-done.6, s32[]{:T(128)S(6)} %select_n.53), kind=kLoop, calls=%fused_computation.60 | loop fusion | flops 2097088 | bytes 2621700 | tf_op jit(solution)/shard_map/reduce_sum | solution.py:321
  44.8 0.7 copy-done.2
  45.6 0.9 fusion.49.x_ref
  46.4 5.8 %shard_map.169 = f32[64,1024]{1,0:T(8,128)} custom-call(s32[1]{0:T(128)} %constant.45.clone.1.start_ref, bf16[64,4096]{1,0:T(8,128)(2,1)} %fusion.49.x_ref, bf16[4096,1024]{1,0:T(8,128)(2,1)} %w_ref.5), custom_call_target="tpu_custom_call" | custom-call | flops 536870912 | bytes 8388608 | tf_op jit(solution)/shard_map/pallas_call | solution.py:53
  52.2 0.9 %dynamic-slice_convert_fusion = bf16[64,512]{1,0:T(8,128)(2,1)S(1)} fusion(f32[64,1024]{1,0:T(8,128)} %shard_map.169, s32[]{:T(128)S(6)} %select_n.63), kind=kLoop, calls=%fused_computation.124 | loop fusion | bytes 131076 | tf_op jit(solution)/shard_map/convert_element_type | solution.py:328
  53.2 1.2 %collective-permute-done.4 = bf16[64,512]{1,0:T(8,128)(2,1)S(1)} collective-permute-done((bf16[64,512]{1,0:T(8,128)(2,1)S(1)}, bf16[64,512]{1,0:T(8,128)(2,1)S(1)}, u32[]{:S(2)}, u32[]{:S(2)}) %collective-permute-start.4) | collective-permute-done | bytes 65568 | tf_op jit(solution)/shard_map/ppermute | solution.py:16
  54.5 1.1 %convolution_convert_fusion = bf16[68,512]{1,0:T(8,128)(2,1)S(1)} fusion(bf16[64,512]{1,0:T(8,128)(2,1)S(1)} %collective-permute-done.4, f32[64,1024]{1,0:T(8,128)} %shard_map.169, s32[]{:T(128)S(6)} %select_n.62, f32[64]{0:T(128)S(1)} %add_rsqrt_fusion, s32[64]{0:T(128)S(1)} %multiply_add_fusion.4, pred[64]{0:T(512)(128)(4,1)S(1)} %broadcast_compare_fusion), kind=kOutput, calls=%fused_computation.58 | convolution fusion | flops 4631040 | bytes 266820 | tf_op jit(solution)/shard_map/dot_general | solution.py:345
  55.6 12.4 %shard_map.170 = (f32[16,4,1024]{2,1,0:T(4,128)S(1)}, f32[3,4,1024]{2,1,0:T(4,128)S(1)}) custom-call(bf16[17,4,512]{2,1,0:T(4,128)(2,1)S(1)} %reshape.77.out_ref), custom_call_target="tpu_custom_call" | custom-call | tf_op jit(solution)/shard_map/pallas_call | solution.py:196
  68.0 0.8 reshape.78
  68.8 1.2 %fusion.73 = (bf16[64,1024]{1,0:T(8,128)(2,1)S(1)}, f32[64,1024]{1,0:T(8,128)S(1)}) fusion(f32[1024]{0:T(1024)S(1)} %get-tuple-element.25, f32[1024]{0:T(1024)S(1)} %get-tuple-element.26, f32[64,1024]{1,0:T(8,128)} %reshape.78, bf16[80,512]{1,0:T(8,128)(2,1)} %copy-done.4, bf16[80,512]{1,0:T(8,128)(2,1)} %copy-done.3), kind=kLoop, calls=%fused_computation.92 | loop fusion | flops 1966080 | bytes 827392 | tf_op jit(solution)/shard_map/convert_element_type | solution.py:41
  70.7 0.9 %add_multiply_fusion = (f32[12,1024]{1,0:T(8,128)S(1)}, f32[12,1024]{1,0:T(8,128)S(1)}, f32[12,1024]{1,0:T(8,128)S(1)}) fusion(f32[1024]{0:T(1024)S(1)} %get-tuple-element.26, f32[12,1024]{1,0:T(8,128)} %reshape.79, bf16[12,1024]{1,0:T(8,128)(2,1)} %collective-permute-done.7), kind=kLoop, calls=%fused_computation.145 | loop fusion | flops 258048 | bytes 225280 | tf_op jit(solution)/shard_map/mul | solution.py:36
  71.6 1.0 %fusion.93 = (bf16[9,1024]{1,0:T(8,128)(2,1)S(1)}, bf16[9,1024]{1,0:T(8,128)(2,1)S(1)}) fusion(f32[16,1024]{1,0:T(8,128)} %convert_element_type.91, f32[16,1024]{1,0:T(8,128)} %get-tuple-element.20, f32[16,1024]{1,0:T(8,128)} %get-tuple-element.19, f32[1024]{0:T(1024)S(1)} %get-tuple-element.25, f32[12,1024]{1,0:T(8,128)S(1)} %get-tuple-element.8, ...), kind=kLoop, calls=%fused_computation.139 | loop fusion | flops 110592 | bytes 262144 | tf_op jit(solution)/shard_map/convert_element_type | solution.py:41
  72.5 3.4 %broadcast_select_fusion.1 = (bf16[1024,512]{1,0:T(8,128)(2,1)S(1)}, bf16[1024,512]{1,0:T(8,128)(2,1)S(1)}) fusion(bf16[1024,512]{1,0:T(8,128)(2,1)} %collective-permute-done.6, pred[]{:T(512)S(6)} %eq.17, f32[512]{0:T(512)S(1)} %get-tuple-element.29, f32[512]{0:T(512)S(1)} %copy-done.11, bf16[1024,512]{1,0:T(8,128)(2,1)S(1)} %copy-done), kind=kLoop, calls=%fused_computation.78 | loop fusion | flops 14680064 | bytes 4198401 | tf_op jit(solution)/shard_map/jit(_where)/select_n | solution.py:24
  76.0 2.5 %fusion.12 = f32[928,512]{1,0:T(8,128)S(1)} fusion(bf16[1024,512]{1,0:T(8,128)(2,1)S(1)} %get-tuple-element.13, bf16[1024,512]{1,0:T(8,128)(2,1)S(1)} %get-tuple-element.14, bf16[7,1024,512]{2,1,0:T(8,128)(2,1)} %param.30), kind=kOutput, calls=%fused_computation.28 | convolution fusion | flops 976879616 | bytes 5046272 | tf_op jit(solution)/shard_map/dot_general | solution.py:296
  78.6 1.1 %fusion.15 = f32[928,512]{1,0:T(8,128)S(1)} fusion(bf16[1024,512]{1,0:T(8,128)(2,1)S(1)} %get-tuple-element.13, bf16[1024,512]{1,0:T(8,128)(2,1)S(1)} %get-tuple-element.14, bf16[7,1024,512]{2,1,0:T(8,128)(2,1)S(1)} %bitcast.66), kind=kOutput, calls=%fused_computation.30 | convolution fusion | flops 976879616 | bytes 5046272 | tf_op jit(solution)/shard_map/dot_general | solution.py:296
  79.7 1.1 %fusion.18 = f32[928,512]{1,0:T(8,128)S(1)} fusion(bf16[1024,512]{1,0:T(8,128)(2,1)S(1)} %get-tuple-element.13, bf16[1024,512]{1,0:T(8,128)(2,1)S(1)} %get-tuple-element.14, bf16[7,1024,512]{2,1,0:T(8,128)(2,1)S(1)} %bitcast.66), kind=kOutput, calls=%fused_computation.32 | convolution fusion | flops 976879616 | bytes 5046272 | tf_op jit(solution)/shard_map/dot_general | solution.py:296
  80.9 1.1 %fusion.21 = f32[928,512]{1,0:T(8,128)S(1)} fusion(bf16[1024,512]{1,0:T(8,128)(2,1)S(1)} %get-tuple-element.13, bf16[1024,512]{1,0:T(8,128)(2,1)S(1)} %get-tuple-element.14, bf16[7,1024,512]{2,1,0:T(8,128)(2,1)S(1)} %bitcast.66), kind=kOutput, calls=%fused_computation.34 | convolution fusion | flops 976879616 | bytes 5046272 | tf_op jit(solution)/shard_map/dot_general | solution.py:296
  82.0 1.1 %fusion.24 = f32[928,512]{1,0:T(8,128)S(1)} fusion(bf16[1024,512]{1,0:T(8,128)(2,1)S(1)} %get-tuple-element.13, bf16[1024,512]{1,0:T(8,128)(2,1)S(1)} %get-tuple-element.14, bf16[7,1024,512]{2,1,0:T(8,128)(2,1)S(1)} %bitcast.66), kind=kOutput, calls=%fused_computation.36 | convolution fusion | flops 976879616 | bytes 5046272 | tf_op jit(solution)/shard_map/dot_general | solution.py:296
  83.1 1.1 %fusion.9 = f32[928,512]{1,0:T(8,128)S(1)} fusion(bf16[1024,512]{1,0:T(8,128)(2,1)S(1)} %get-tuple-element.13, bf16[1024,512]{1,0:T(8,128)(2,1)S(1)} %get-tuple-element.14, bf16[7,1024,512]{2,1,0:T(8,128)(2,1)S(1)} %bitcast.66), kind=kOutput, calls=%fused_computation.26 | convolution fusion | flops 976879616 | bytes 5046272 | tf_op jit(solution)/shard_map/dot_general | solution.py:296
  85.5 1.3 %fusion.46 = bf16[96,512]{1,0:T(8,128)(2,1)S(1)} fusion(bf16[7168,512]{1,0:T(8,128)(2,1)S(1)} %bitcast.67, bf16[16,7168]{1,0:T(8,128)(2,1)S(1)} %slice_dynamic-update-slice_fusion.3, bf16[80,7168]{1,0:T(8,128)(2,1)S(1)} %fusion.84, f32[16,512]{1,0:T(8,128)S(1)} %copy-done.10, f32[16,512]{1,0:T(8,128)S(1)} %copy-done.9, ...), kind=kOutput, calls=%fused_computation.57 | convolution fusion | flops 707641344 | bytes 9013248 | tf_op jit(solution)/shard_map/dot_general | solution.py:362
  86.9 1.7 %fusion.35 = bf16[928,512]{1,0:T(8,128)(2,1)S(1)} fusion(f32[928,512]{1,0:T(8,128)S(1)} %fusion.9, f32[928,512]{1,0:T(8,128)S(1)} %fusion.24, f32[928,512]{1,0:T(8,128)S(1)} %fusion.21, f32[928,512]{1,0:T(8,128)S(1)} %fusion.18, f32[928,512]{1,0:T(8,128)S(1)} %fusion.15, f32[928,512]{1,0:T(8,128)S(1)} %fusion.12, ...), kind=kOutput, calls=%fused_computation.48 | convolution fusion | flops 981155840 | bytes 17401856 | tf_op jit(solution)/shard_map/dot_general | solution.py:296
  88.5 1.0 %pad_maximum_fusion.2 = bf16[1024,512]{1,0:T(8,128)(2,1)} fusion(bf16[16,512]{1,0:T(8,128)(2,1)S(1)} %slice.213, bf16[928,512]{1,0:T(8,128)(2,1)S(1)} %fusion.35, bf16[80,512]{1,0:T(8,128)(2,1)S(1)} %slice.199), kind=kLoop, calls=%fused_computation.61 | loop fusion | flops 3145728 | bytes 2097152 | tf_op jit(solution)/shard_map/concatenate | solution.py:364
  (105 shorter events, 7.8 us)
Async XLA Ops:
  0.6 31.7 %collective-permute-start.3 = (f32[512]{0:T(512)}, f32[512]{0:T(512)S(1)}, u32[]{:S(2)}, u32[]{:S(2)}) collective-permute-start(f32[512]{0:T(512)} %param.29), channel_id=1, source_target_pairs={{0,1},{1,0},{2,3},{3,2},{4,5},{5,4},{6,7},{7,6},{8,9},{9,8},{10,11... | collective-permute-start | bytes 6152 | tf_op jit(solution)/shard_map/ppermute | solution.py:16
  2.5 4.8 %copy-start.15 = (s32[64]{0:T(128)S(1)}, s32[64]{0:T(128)}, u32[]{:S(2)}) copy-start(s32[64]{0:T(128)} %param.21) | copy-start | bytes 772
  2.5 4.9 %copy-start.5 = (bf16[64,2048]{1,0:T(8,128)(2,1)S(1)}, bf16[64,2048]{1,0:T(8,128)(2,1)}, u32[]{:S(2)}) copy-start(bf16[64,2048]{1,0:T(8,128)(2,1)} %param.16) | copy-start | bytes 786436
  2.6 4.9 %copy-start.8 = (bf16[64,2048]{1,0:T(8,128)(2,1)S(1)}, bf16[64,2048]{1,0:T(8,128)(2,1)}, u32[]{:S(2)}) copy-start(bf16[64,2048]{1,0:T(8,128)(2,1)} %param.17) | copy-start | bytes 786436
  7.1 1.5 %copy-start.7 = (bf16[64,2048]{1,0:T(8,128)(2,1)S(1)}, bf16[64,2048]{1,0:T(8,128)(2,1)}, u32[]{:S(2)}) copy-start(bf16[64,2048]{1,0:T(8,128)(2,1)} %param.18) | copy-start | bytes 786436
  13.2 8.5 %copy-start = (bf16[1024,512]{1,0:T(8,128)(2,1)S(1)}, bf16[1024,512]{1,0:T(8,128)(2,1)}, u32[]{:S(2)}) copy-start(bf16[1024,512]{1,0:T(8,128)(2,1)} %param.28) | copy-start | bytes 3145732
  13.2 9.7 %copy-start.16 = (s32[64]{0:T(128)S(1)}, s32[64]{0:T(128)}, u32[]{:S(2)}) copy-start(s32[64]{0:T(128)} %param.26) | copy-start | bytes 772
  13.2 9.7 %copy-start.14 = (s32[64]{0:T(128)S(1)}, s32[64]{0:T(128)}, u32[]{:S(2)}) copy-start(s32[64]{0:T(128)} %param.27) | copy-start | bytes 772
  21.6 21.7 %collective-permute-start = (bf16[64,4096]{1,0:T(8,128)(2,1)}, bf16[64,4096]{1,0:T(8,128)(2,1)}, u32[]{:S(2)}, u32[]{:S(2)}) collective-permute-start(bf16[64,4096]{1,0:T(8,128)(2,1)} %shard_map.168), channel_id=1, source_target_pairs={{0,1},{1,0},{2,3},{3,2},{4,5},{5,4},{6,7},{7,6},{8,9},{9,8},{10,11... | collective-permute-start | bytes 1572872 | tf_op jit(solution)/shard_map/ppermute | solution.py:16
  21.7 13.5 %collective-permute-start.1 = (bf16[80,512]{1,0:T(8,128)(2,1)S(1)}, bf16[80,512]{1,0:T(8,128)(2,1)S(1)}, u32[]{:S(2)}, u32[]{:S(2)}) collective-permute-start(bf16[80,512]{1,0:T(8,128)(2,1)S(1)} %pad_maximum_fusion.8), channel_id=1, source_target_pairs={{0,1},{1,0},{2,3},{3,2},{4,5},{5,4},{6,7},{7,6},{8,9},{9,8},{10,11... | collective-permute-start | bytes 245768 | tf_op jit(solution)/shard_map/ppermute | solution.py:16
  31.6 0.7 copy-start.13
  31.6 0.7 copy-start.11
  32.3 11.0 %copy-start.1 = (f32[64,4096]{1,0:T(8,128)S(1)}, f32[64,4096]{1,0:T(8,128)}, u32[]{:S(2)}) copy-start(f32[64,4096]{1,0:T(8,128)} %shard_map.167) | copy-start | bytes 3145732
  32.3 11.0 %copy-start.6 = (bf16[64,8192]{1,0:T(8,128)(2,1)S(1)}, bf16[64,8192]{1,0:T(8,128)(2,1)}, u32[]{:S(2)}) copy-start(bf16[64,8192]{1,0:T(8,128)(2,1)} %param.22) | copy-start | bytes 3145732
  35.1 37.4 %collective-permute-start.6 = (bf16[1024,512]{1,0:T(8,128)(2,1)}, bf16[1024,512]{1,0:T(8,128)(2,1)}, u32[]{:S(2)}, u32[]{:S(2)}) collective-permute-start(bf16[1024,512]{1,0:T(8,128)(2,1)} %fusion.3), channel_id=1, source_target_pairs={{0,1},{1,0},{2,3},{3,2},{4,5},{5,4},{6,7},{7,6},{8,9},{9,8},{10,11... | collective-permute-start | bytes 3145736 | tf_op jit(solution)/shard_map/ppermute | solution.py:16
  35.2 17.0 %copy-start.3 = (bf16[80,512]{1,0:T(8,128)(2,1)}, bf16[80,512]{1,0:T(8,128)(2,1)S(1)}, u32[]{:S(2)}) copy-start(bf16[80,512]{1,0:T(8,128)(2,1)S(1)} %get-tuple-element.17) | copy-start | bytes 245764
  35.2 17.0 %copy-start.4 = (bf16[80,512]{1,0:T(8,128)(2,1)}, bf16[80,512]{1,0:T(8,128)(2,1)S(1)}, u32[]{:S(2)}) copy-start(bf16[80,512]{1,0:T(8,128)(2,1)S(1)} %get-tuple-element.18) | copy-start | bytes 245764
  35.2 6.8 %collective-permute-start.2 = (bf16[16,1024]{1,0:T(8,128)(2,1)S(1)}, bf16[16,1024]{1,0:T(8,128)(2,1)S(1)}, u32[]{:S(2)}, u32[]{:S(2)}) collective-permute-start(bf16[16,1024]{1,0:T(8,128)(2,1)S(1)} %pad_maximum_fusion.11), channel_id=1, source_target_pairs={{0,2},{2,4},{4,6},{6,8},{8,10},{10,12},{12,14},{14,16},{16,18},{18... | collective-permute-start | bytes 98312 | tf_op jit(solution)/shard_map/ppermute | solution.py:288
  40.7 29.9 %collective-permute-start.7 = (bf16[12,1024]{1,0:T(8,128)(2,1)}, bf16[12,1024]{1,0:T(8,128)(2,1)}, u32[]{:S(2)}, u32[]{:S(2)}) collective-permute-start(bf16[12,1024]{1,0:T(8,128)(2,1)} %pad_maximum_fusion.10), channel_id=1, source_target_pairs={{2,0},{4,2},{6,4},{8,6},{10,8},{12,10},{14,12},{16,14},{18,16},{20... | collective-permute-start | bytes 73736 | tf_op jit(solution)/shard_map/ppermute | solution.py:289
  44.8 0.8 copy-start.2
  44.8 8.5 %collective-permute-start.5 = (f32[64]{0:T(128)S(1)}, f32[64]{0:T(128)S(1)}, u32[]{:S(2)}, u32[]{:S(2)}) collective-permute-start(f32[64]{0:T(128)S(1)} %get-tuple-element.11), channel_id=1, source_target_pairs={{0,1},{1,0},{2,3},{3,2},{4,5},{5,4},{6,7},{7,6},{8,9},{9,8},{10,11... | collective-permute-start | bytes 776 | tf_op jit(solution)/shard_map/ppermute | solution.py:16
  53.1 1.3 %collective-permute-start.4 = (bf16[64,512]{1,0:T(8,128)(2,1)S(1)}, bf16[64,512]{1,0:T(8,128)(2,1)S(1)}, u32[]{:S(2)}, u32[]{:S(2)}) collective-permute-start(bf16[64,512]{1,0:T(8,128)(2,1)S(1)} %dynamic-slice_convert_fusion), channel_id=1, source_target_pairs={{0,1},{1,0},{2,3},{3,2},{4,5},{5,4},{6,7},{7,6},{8,9},{9,8},{10,11... | collective-permute-start | bytes 196616 | tf_op jit(solution)/shard_map/ppermute | solution.py:16
  72.5 6.0 %slice-start = ((s8[7340032]{0:T(1024)(128)(4,1)}), s8[4194304]{0:T(1024)(128)(4,1)S(1)}, s32[]{:S(2)}) async-start(s8[7340032]{0:T(1024)(128)(4,1)} %bitcast.65), calls=%async_computation | async-start | bytes 8388608
  76.0 2.5 %slice-start.1 = ((s8[7340032]{0:T(1024)(128)(4,1)}), s8[3145728]{0:T(1024)(128)(4,1)S(1)}, s32[]{:S(2)}) async-start(s8[7340032]{0:T(1024)(128)(4,1)} %bitcast.65), calls=%async_computation.1 | async-start | bytes 6291456
  84.8 0.8 copy-start.9
  84.8 0.8 copy-start.10
  84.8 0.8 copy-start.12
